TPU v7x, 128 devices: a whole 4x4x4 slice. The times are simulated.
128 devices in a mesh: gx: 16 (over z, x), gy: 8 (over y, core).
Axes of the slice: x: 4, y: 4, z: 4, core: 2. Of those that a mesh axis runs over, the one named last changes fastest.
Arguments:
- cotangent: float32 [16, 8, 42, 1024], P('gx', 'gy'), may hold values from -6 to 6
- section_states: bfloat16 [3, 16, 8, 42, 1024], P(None, 'gx', 'gy'), may hold values from -6 to 6
- inverse_area: float32 [16, 8, 1024], P('gx', 'gy'), may hold values from 0.5 to 2
- edge_length: float32 [16, 8, 3, 1024], P('gx', 'gy'), may hold values from 0.5 to 1.5
- roughness: float32 [16, 8, 1024], P('gx', 'gy'), may hold values from 0.5 to 2
- soil_conductance: float32 [16, 8, 1024], P('gx', 'gy'), may hold values from 0.5 to 2
- zone_friction: float32 [512], replicated, may hold values from 0.25 to 1
- zone_conductivity: float32 [512], replicated, may hold values from 0.25 to 1
- wet_mask: int32 [16, 8, 1024], P('gx', 'gy'), may hold values 0 or 1
- element_zone: int32 [16, 8, 1024], P('gx', 'gy'), may hold values from 0 to 511, as said below
- send_face: int32 [16, 8, 8, 256], P('gx', 'gy'), may hold values from 0 to 3071, as said below
- send_count: int32 [16, 8, 8], P('gx', 'gy'), may hold values from 0 to 256, as said below
- face_partner: int32 [16, 8, 3, 1024], P('gx', 'gy'), may hold values from 0 to 4867, as said below
- volume_matrix: float32 [12, 12], replicated, may hold values from -1.75 to 1.75
- flux_in: float32 [8, 8], replicated, may hold values from -2 to 2
- flux_out: float32 [8, 8], replicated, may hold values from -2 to 2
Outputs:
- adjoint: float32 [16, 8, 42, 1024], P('gx', 'gy')
- zone_grads: float32 [2, 512], replicated
Inputs may be any that keep to these rules, and one draw needn't show every extreme that they name: `element_zone`: zones lie near their partition: an element of partition (a, b) has a zone among the 8 zones from (a*8+b)*4 on, modulo 512. send_count[a, b, n] equals send_count of the partition at offset n for offset 7 - n; it is 0 where that partition lies outside the grid, 1 to 4 for the four diagonal offsets (4 for some pair in every draw), at least 192 for the others, and 256 for some pair in every draw. `send_face`: the live slots of a partition name distinct faces; slots at or beyond the count hold 0. `face_partner`: the faces are paired: a face sent in slot j to offset n faces entry 3072 + n*256 + j, the other faces face a local face whose partner they are, or themselves.
All inputs are finite; a program needn't handle non-finite values. No bound on the sum of `wet_mask` on one device may be relied on, other than what follows from the above.
Results may differ from a plain program's by a relative error of at most 0.0003.
Values may be sent and summed in bfloat16 or wider, within the bound.
A program may use at most 64 MiB of HBM per device.

v0:
```python
import jax
import jax.numpy as jnp
import numpy as np
from jax import lax
from jax.sharding import PartitionSpec as P

LAYERS = 10
ZONE_DEV = 4
TIME_STEP = 0.2
SALT_RETURN = 0.5
LATERAL = 0.5
GRAD_WEIGHT = 1.0 / 64.0
FACE_NODES = ((1, 2), (2, 0), (0, 1))
MOMENTUM_ROWS = np.array([0, 0, 0, 1, 1, 1, 1, 1, 1, 0, 0, 0], np.float32)


def shifted(x, axis, by):
    peers = lax.axis_size(axis)
    pairs = [(i, i + by) for i in range(peers) if 0 <= i + by < peers]
    return lax.ppermute(x, axis, pairs)


def trace_rows():
    channels = 8 + 2 * LAYERS
    rows = np.zeros((channels, 3), np.int32)
    for face_no in range(3):
        for end_no in range(2):
            node_no = FACE_NODES[face_no][end_no]
            for comp_no in range(4):
                rows[comp_no * 2 + end_no, face_no] = comp_no * 3 + node_no
            for layer_no in range(LAYERS):
                rows[8 + layer_no * 2 + end_no, face_no] = 12 + layer_no * 3 + node_no
    return rows.reshape(-1)


def take_traces(state, rows):
    channels = rows.shape[0] // 3
    return state[rows].reshape(channels, 3 * state.shape[1])


def lift_back(flux, rows, row_count):
    return jnp.zeros((row_count, flux.shape[-1]), jnp.float32).at[rows].add(flux)


def section_speed(flat_traces, outer_flat):
    return jnp.sqrt(1.0 + 0.25 * jnp.mean(flat_traces[:8] ** 2 + outer_flat[:8] ** 2, axis=0))


def local_operator(
    state,
    received,
    conductivity,
    friction,
    wave_speed,
    inverse_area,
    edge_length,
    wet_mask,
    partner,
    volume_matrix,
    flux_in,
    flux_out,
    rows,
):
    element_count = state.shape[1]
    channels = rows.shape[0] // 3
    flat_traces = take_traces(state, rows)
    trace_table = jnp.concatenate([flat_traces, received.reshape(channels, -1)], axis=1)
    outer_traces = trace_table[:, partner.reshape(-1)].reshape(channels, 3, element_count)
    inner_traces = flat_traces.reshape(channels, 3, element_count)
    surf_inner = inner_traces[:8]
    surf_outer = outer_traces[:8]
    flux_surface = (
        jnp.einsum("ab,bfe->afe", flux_in, surf_inner, precision=lax.Precision.HIGHEST)
        - jnp.einsum("ab,bfe->afe", flux_out, surf_outer, precision=lax.Precision.HIGHEST)
        + 0.5 * wave_speed[None] * (surf_inner - surf_outer)
    )
    flux_pore = LATERAL * conductivity[None, None] * (outer_traces[8:] - inner_traces[8:])
    flux_all = jnp.concatenate([flux_surface, flux_pore], axis=0) * edge_length[None]
    lifted = lift_back(flux_all.reshape(channels * 3, element_count), rows, state.shape[0])
    volume = jnp.dot(volume_matrix, state[:12], precision=lax.Precision.HIGHEST)
    top_exchange = conductivity[None] * (state[9:12] - state[12:15])
    momentum = jnp.asarray(MOMENTUM_ROWS, dtype=jnp.float32)[:, None]
    surface = inverse_area[None] * (volume + lifted[:12]) - momentum * friction[None] * state[:12]
    surface = (
        jnp.concatenate([surface[:9], surface[9:12] - SALT_RETURN * top_exchange], axis=0)
        * wet_mask[None]
    )
    layers = state[12:].reshape(LAYERS, 3, element_count)
    between = conductivity[None, None] * (layers[:-1] - layers[1:])
    from_above = jnp.concatenate([top_exchange[None], between], axis=0)
    to_below = jnp.concatenate([between, jnp.zeros((1, 3, element_count), jnp.float32)], axis=0)
    pore = (from_above - to_below).reshape(3 * LAYERS, element_count) + inverse_area[None] * lifted[
        12:
    ]
    return jnp.concatenate([surface, pore], axis=0)


def forward_estuary(block, by_count):
    return shifted(block, "gx", by_count)


def forward_across(block, by_count):
    return shifted(block, "gy", by_count)


def backward_estuary(block, by_count):
    return shifted(block, "gx", by_count)


def backward_across(block, by_count):
    return shifted(block, "gy", by_count)


def route_blocks(blocks, estuary_hop, across_hop):
    pieces = [
        across_hop(estuary_hop(blocks[..., 7, :], 1), 1),
        estuary_hop(blocks[..., 6, :], 1),
        across_hop(estuary_hop(blocks[..., 5, :], 1), -1),
        across_hop(blocks[..., 4, :], 1),
        across_hop(blocks[..., 3, :], -1),
        across_hop(estuary_hop(blocks[..., 2, :], -1), 1),
        estuary_hop(blocks[..., 1, :], -1),
        across_hop(estuary_hop(blocks[..., 0, :], -1), -1),
    ]
    return jnp.stack(pieces, axis=-2)


def local(
    cotangent,
    section_states,
    inverse_area,
    edge_length,
    roughness,
    soil_conductance,
    zone_friction,
    zone_conductivity,
    wet_mask,
    element_zone,
    send_face,
    send_count,
    face_partner,
    volume_matrix,
    flux_in,
    flux_out,
):
    rows = jnp.asarray(trace_rows(), dtype=jnp.int32)
    channels = rows.shape[0] // 3
    cotangent_local = cotangent[0, 0]
    row_count = cotangent_local.shape[0]
    element_count = cotangent_local.shape[1]
    area_local = inverse_area[0, 0]
    edges_local = edge_length[0, 0]
    rough_local = roughness[0, 0]
    conduct_local = soil_conductance[0, 0]
    wetness = wet_mask[0, 0].astype(jnp.float32)
    zones_local = element_zone[0, 0]
    faces_sent = send_face[0, 0]
    counts_sent = send_count[0, 0]
    partner = face_partner[0, 0]
    zone_total = zone_friction.shape[0]
    conductivity = zone_conductivity[zones_local] * conduct_local
    zone_factor = zone_friction[zones_local]
    slot_index = jnp.arange(faces_sent.shape[1])
    live_slots = (slot_index[None, :] < counts_sent[:, None]).astype(jnp.float32)
    device_number = lax.axis_index("gx") * lax.axis_size("gy") + lax.axis_index("gy")
    zone_base = device_number * ZONE_DEV
    near_count = 2 * ZONE_DEV
    offset_zone = (zones_local - zone_base) % zone_total
    near_onehot = (offset_zone[None, :] == jnp.arange(near_count, dtype=jnp.int32)[:, None]).astype(
        jnp.float32
    )
    near_ids = (zone_base + jnp.arange(near_count, dtype=jnp.int32)) % zone_total
    forward_all = section_states[:, 0, 0].astype(jnp.float32)

    def section_received(states):
        flat_states = jax.vmap(lambda one: take_traces(one, rows))(states)
        outgoing = (flat_states[:, :, faces_sent] * live_slots[None, None]).astype(jnp.bfloat16)
        return route_blocks(outgoing, forward_estuary, forward_across).astype(jnp.float32)

    def received_of(section_no):
        return section_received(forward_all[section_no : section_no + 1])[0]

    def section_adjoint(section_no, weight_field):
        forward_state = forward_all[section_no]
        flat_forward = take_traces(forward_state, rows)
        received = received_of(section_no)
        trace_table = jnp.concatenate([flat_forward, received.reshape(channels, -1)], axis=1)
        outer_forward = trace_table[:, partner.reshape(-1)]
        wave_speed = section_speed(flat_forward, outer_forward).reshape(3, element_count)
        moment = jnp.sqrt(1.0 + jnp.mean(forward_state[3:9] ** 2, axis=0))
        friction_base = rough_local * moment
        friction = zone_factor * friction_base

        def section_operator(state, incoming, conduct_in, friction_in):
            return local_operator(
                state,
                incoming,
                conduct_in,
                friction_in,
                wave_speed,
                area_local,
                edges_local,
                wetness,
                partner,
                volume_matrix,
                flux_in,
                flux_out,
                rows,
            )

        unused, pullback = jax.vjp(
            section_operator, forward_state, received, conductivity, friction
        )
        state_bar, received_bar, conduct_bar, friction_bar = pullback(TIME_STEP * weight_field)
        returned = route_blocks(received_bar, backward_estuary, backward_across)
        flat_bar = (
            jnp.zeros((channels, 3 * element_count), jnp.float32)
            .at[:, faces_sent]
            .add(returned * live_slots[None])
        )
        state_bar = state_bar + lift_back(
            flat_bar.reshape(channels * 3, element_count), rows, row_count
        )
        element_terms = jnp.stack(
            [friction_base * friction_bar, conduct_local * conduct_bar], axis=0
        )
        near_terms = jnp.einsum(
            "ke,ze->kz", element_terms, near_onehot, precision=lax.Precision.HIGHEST
        )
        zone_terms = jnp.zeros((2, zone_total), jnp.float32).at[:, near_ids].add(near_terms)
        return (state_bar, zone_terms)

    bar_two, terms_two = section_adjoint(2, cotangent_local)
    lam_two = 2.0 / 3.0 * (cotangent_local + bar_two)
    bar_one, terms_one = section_adjoint(1, lam_two)
    lam_one = 0.25 * (lam_two + bar_one)
    bar_zero, terms_zero = section_adjoint(0, lam_one)
    adjoint = cotangent_local / 3.0 + 0.75 * lam_two + lam_one + bar_zero
    summed = [lax.psum(terms, ("gx", "gy")) for terms in (terms_two, terms_one, terms_zero)]
    zone_grads = GRAD_WEIGHT * (2.0 / 3.0 * summed[0] + 0.25 * summed[1] + summed[2])
    return (adjoint[None, None], zone_grads)


def solution(mesh):
    placed = (
        P("gx", "gy", None, None),
        P(None, "gx", "gy", None, None),
        P("gx", "gy", None),
        P("gx", "gy", None, None),
        P("gx", "gy", None),
        P("gx", "gy", None),
        P(),
        P(),
        P("gx", "gy", None),
        P("gx", "gy", None),
        P("gx", "gy", None, None),
        P("gx", "gy", None),
        P("gx", "gy", None, None),
        P(),
        P(),
        P(),
    )
    return jax.shard_map(
        local,
        mesh=mesh,
        in_specs=placed,
        out_specs=(P("gx", "gy", None, None), P()),
        check_vma=False,
    )
```

profile of v0, /device:TPU:41, one launch (start us, length us, event | category | flops | bytes accessed | tf_op | source)
XLA Modules:
  0.0 641.6 jit_solution(15260128408146421137)
XLA Ops:
  5.4 7.6 %gather_fusion.12 = f32[2048,28]{1,0:T(8,128)} fusion(f32[28,3072]{0,1:T(8,128)S(1)} %copy.369, s32[2048]{0:T(1024)S(1)} %broadcast_clamp_fusion.1), kind=kCustom, calls=%fused_computation.15 | custom fusion | bytes 466944 | tf_op jit(solution)/shard_map/gather | solution.py:177
  13.0 2.3 copy.370
  17.5 7.6 %gather_fusion.8 = f32[2048,28]{1,0:T(8,128)} fusion(f32[28,3072]{0,1:T(8,128)S(1)} %copy.340, s32[2048]{0:T(1024)S(1)} %broadcast_clamp_fusion.1), kind=kCustom, calls=%fused_computation.10 | custom fusion | bytes 466944 | tf_op jit(solution)/shard_map/gather | solution.py:177
  25.1 2.3 copy.341
  29.0 7.6 %gather_fusion.4 = f32[2048,28]{1,0:T(8,128)} fusion(f32[28,3072]{0,1:T(8,128)S(1)} %copy.311, s32[2048]{0:T(1024)S(1)} %broadcast_clamp_fusion.1), kind=kCustom, calls=%fused_computation.5 | custom fusion | bytes 466944 | tf_op jit(solution)/shard_map/gather | solution.py:177
  40.8 3.1 collective-permute-start
  43.9 3.1 collective-permute-start.2
  47.0 2.8 collective-permute-start.3
  49.9 4.6 collective-permute-start.5
  59.3 6.9 %gather_fusion = f32[1024]{0:T(1024)S(1)} fusion(f32[512]{0:T(512)S(1)} %copy-done.1, s32[1024]{0:T(1024)S(1)} %broadcast_clamp_fusion.2), kind=kCustom, calls=%fused_computation | custom fusion | bytes 12288 | tf_op jit(solution)/shard_map/gather | solution.py:161
  66.2 6.9 %gather_fusion.1 = f32[1024]{0:T(1024)S(1)} fusion(f32[512]{0:T(512)S(1)} %copy-done.2, s32[1024]{0:T(1024)S(1)} %broadcast_clamp_fusion.2), kind=kCustom, calls=%fused_computation.1 | custom fusion | bytes 12288 | tf_op jit(solution)/shard_map/gather | solution.py:162
  82.1 4.6 collective-permute-start.7
  86.7 2.2 collective-permute-start.9
  89.4 2.2 collective-permute-start.10
  91.6 3.1 collective-permute-start.26
  94.7 4.8 collective-permute-start.29
  101.5 4.3 collective-permute-start.33
  107.7 3.9 collective-permute-start.53
  113.6 5.8 collective-permute-start.57
  119.4 3.9 collective-permute-start.1
  129.8 3.6 collective-permute-start.8
  150.4 5.5 collective-permute-start.31
  156.6 3.4 collective-permute-start.34
  162.7 4.5 collective-permute-start.25
  167.2 2.1 collective-permute-start.28
  172.6 10.9 %gather_fusion.5 = f32[3072,28]{1,0:T(8,128)} fusion(f32[28,5120]{0,1:T(8,128)S(1)} %copy.321, s32[3072]{0:T(1024)S(1)} %copy-done.60), kind=kCustom, calls=%fused_computation.6 | custom fusion | bytes 700416 | tf_op jit(solution)/shard_map/gather | solution.py:188
  190.1 17.9 %scatter_custom_fusion = f32[28,5120]{0,1:T(8,128)S(1)} fusion(s32[3072]{0:T(1024)} %bitcast.397, f32[3072,28]{1,0:T(8,128)} %copy.327, f32[]{:T(128)} %constant.38.clone.1), kind=kCustom, calls=%fused_computation.36 | custom fusion | flops 86016 | bytes 573952 | tf_op jit(solution)/shard_map/transpose(jvp())/scatter-add | solution.py:68
  209.8 2.0 collective-permute-start.51
  211.8 5.5 collective-permute-start.55
  217.3 3.4 collective-permute-start.58
  220.7 4.5 collective-permute-start.32
  232.1 3.6 collective-permute-start.49
  237.7 3.6 collective-permute-start.56
  249.4 11.9 %gather_fusion.9 = f32[3072,28]{1,0:T(8,128)} fusion(f32[28,5120]{0,1:T(8,128)S(1)} %copy.350, s32[3072]{0:T(1024)} %broadcast_clamp_fusion), kind=kCustom, calls=%fused_computation.11 | custom fusion | bytes 700416 | tf_op jit(solution)/shard_map/gather | solution.py:188
  269.5 2.9 collective-permute-start.15
  273.2 4.5 collective-permute-start.17
  284.4 11.9 %gather_fusion.13 = f32[3072,28]{1,0:T(8,128)} fusion(f32[28,5120]{0,1:T(8,128)S(1)} %copy.379, s32[3072]{0:T(1024)} %broadcast_clamp_fusion), kind=kCustom, calls=%fused_computation.16 | custom fusion | bytes 700416 | tf_op jit(solution)/shard_map/gather | solution.py:188
  298.6 4.2 collective-permute-start.19
  302.8 3.6 collective-permute-start.22
  307.2 3.4 collective-permute-start.21
  310.5 4.5 collective-permute-start.13
  317.0 3.6 collective-permute-start.20
  320.6 2.1 collective-permute-start.23
  336.6 13.9 %scatter_custom_fusion.2 = f32[28,3072]{0,1:T(8,128)S(1)} fusion(s32[2048]{0:T(1024)} %bitcast.407, f32[2048,28]{1,0:T(8,128)} %bitcast.370, f32[]{:T(128)} %constant.38.clone.1), kind=kCustom, calls=%fused_computation.57 | custom fusion | flops 57344 | bytes 344576 | tf_op jit(solution)/shard_map/scatter-add | solution.py:219
  363.1 17.9 %scatter_custom_fusion.4 = f32[28,5120]{0,1:T(8,128)S(1)} fusion(s32[3072]{0:T(1024)} %bitcast.398, f32[3072,28]{1,0:T(8,128)} %copy.356, f32[]{:T(128)} %constant.38.clone.1), kind=kCustom, calls=%fused_computation.34 | custom fusion | flops 86016 | bytes 573952 | tf_op jit(solution)/shard_map/transpose(jvp())/scatter-add | solution.py:68
  390.9 3.0 collective-permute-start.39
  395.5 4.4 collective-permute-start.41
  402.9 2.3 fusion.116
  410.2 4.2 collective-permute-start.43
  414.4 4.0 collective-permute-start.46
  420.9 3.3 collective-permute-start.45
  424.2 4.5 collective-permute-start.37
  430.7 3.6 collective-permute-start.44
  448.8 13.6 %scatter_custom_fusion.6 = f32[28,3072]{0,1:T(8,128)S(1)} fusion(s32[2048]{0:T(1024)} %bitcast.408, f32[2048,28]{1,0:T(8,128)S(1)} %bitcast.371, f32[]{:T(128)} %constant.38.clone.1), kind=kCustom, calls=%fused_computation.55 | custom fusion | flops 57344 | bytes 344576 | tf_op jit(solution)/shard_map/scatter-add | solution.py:219
  474.9 17.9 %scatter_custom_fusion.8 = f32[28,5120]{0,1:T(8,128)S(1)} fusion(s32[3072]{0:T(1024)} %bitcast.399, f32[3072,28]{1,0:T(8,128)} %copy.385, f32[]{:T(128)} %constant.38.clone.1), kind=kCustom, calls=%fused_computation.32 | custom fusion | flops 86016 | bytes 573952 | tf_op jit(solution)/shard_map/transpose(jvp())/scatter-add | solution.py:68
  502.7 2.8 collective-permute-start.63
  506.3 4.4 collective-permute-start.65
  510.8 2.1 collective-permute-start.66
  518.1 69.9 %all-reduce.42 = (f32[2,512]{0,1:T(8,128)}, f32[2,512]{0,1:T(8,128)}, f32[2,512]{0,1:T(8,128)}) all-reduce(f32[2,512]{0,1:T(8,128)S(1)} %scatter_custom_fusion.14, f32[2,512]{0,1:T(8,128)S(1)} %scatter_custom_fusion.13, f32[2,512]{0,1:T(8,128)} %scatter_custom_fusion.12), channel_id=1, replica_groups=mesh['gx'=16,'gy'=8] {'gx','gy'}, use_global_device_ids=true, to_apply=%region_35.36 | all-reduce | flops 3072 | bytes 24576 | tf_op jit(solution)/shard_map/psum | solution.py:239
  593.3 4.3 collective-permute-start.67
  602.0 2.7 collective-permute-start.69
  604.7 3.1 collective-permute-start.61
  609.7 3.6 collective-permute-start.68
  624.9 13.6 %scatter_custom_fusion.10 = f32[28,3072]{0,1:T(8,128)S(1)} fusion(s32[2048]{0:T(1024)} %bitcast.409, f32[2048,28]{1,0:T(8,128)S(1)} %bitcast.369, f32[]{:T(128)} %constant.38.clone.1), kind=kCustom, calls=%fused_computation.53 | custom fusion | flops 57344 | bytes 344576 | tf_op jit(solution)/shard_map/scatter-add | solution.py:219
  (692 shorter events, 225.0 us)
Async XLA Ops:
  40.8 41.3 %collective-permute-start = (bf16[1,28,256]{2,1,0:T(8,128)(2,1)}, bf16[1,28,256]{2,1,0:T(8,128)(2,1)}, u32[]{:S(2)}, u32[]{:S(2)}) collective-permute-start(bf16[1,28,256]{2,1,0:T(8,128)(2,1)} %get-tuple-element.115), channel_id=1, source_target_pairs={{0,8},{8,16},{16,24},{24,32},{32,40},{40,48},{48,56},{56,64},{64,7... | collective-permute-start | bytes 43016 | tf_op jit(solution)/shard_map/ppermute | solution.py:20
  43.9 42.7 %collective-permute-start.2 = (bf16[1,28,256]{2,1,0:T(8,128)(2,1)}, bf16[1,28,256]{2,1,0:T(8,128)(2,1)}, u32[]{:S(2)}, u32[]{:S(2)}) collective-permute-start(bf16[1,28,256]{2,1,0:T(8,128)(2,1)} %get-tuple-element.114), channel_id=1, source_target_pairs={{0,8},{8,16},{16,24},{24,32},{32,40},{40,48},{48,56},{56,64},{64,7... | collective-permute-start | bytes 43016 | tf_op jit(solution)/shard_map/ppermute | solution.py:20
  47.0 42.4 %collective-permute-start.3 = (bf16[1,28,256]{2,1,0:T(8,128)(2,1)}, bf16[1,28,256]{2,1,0:T(8,128)(2,1)}, u32[]{:S(2)}, u32[]{:S(2)}) collective-permute-start(bf16[1,28,256]{2,1,0:T(8,128)(2,1)} %get-tuple-element.113), channel_id=1, source_target_pairs={{0,8},{8,16},{16,24},{24,32},{32,40},{40,48},{48,56},{56,64},{64,7... | collective-permute-start | bytes 43016 | tf_op jit(solution)/shard_map/ppermute | solution.py:20
  49.9 41.7 %collective-permute-start.5 = (bf16[1,28,256]{2,1,0:T(8,128)(2,1)}, bf16[1,28,256]{2,1,0:T(8,128)(2,1)}, u32[]{:S(2)}, u32[]{:S(2)}) collective-permute-start(bf16[1,28,256]{2,1,0:T(8,128)(2,1)} %get-tuple-element.112), channel_id=1, source_target_pairs={{0,1},{1,2},{2,3},{3,4},{4,5},{5,6},{6,7},{8,9},{9,10},{10,11},{11... | collective-permute-start | bytes 43016 | tf_op jit(solution)/shard_map/ppermute | solution.py:20
  54.5 40.3 %collective-permute-start.6 = (bf16[1,28,256]{2,1,0:T(8,128)(2,1)}, bf16[1,28,256]{2,1,0:T(8,128)(2,1)}, u32[]{:S(2)}, u32[]{:S(2)}) collective-permute-start(bf16[1,28,256]{2,1,0:T(8,128)(2,1)} %get-tuple-element.111), channel_id=1, source_target_pairs={{1,0},{2,1},{3,2},{4,3},{5,4},{6,5},{7,6},{9,8},{10,9},{11,10},{12... | collective-permute-start | bytes 43016 | tf_op jit(solution)/shard_map/ppermute | solution.py:20
  82.1 17.4 %collective-permute-start.7 = (bf16[1,28,256]{2,1,0:T(8,128)(2,1)S(1)}, bf16[1,28,256]{2,1,0:T(8,128)(2,1)}, u32[]{:S(2)}, u32[]{:S(2)}) collective-permute-start(bf16[1,28,256]{2,1,0:T(8,128)(2,1)S(1)} %copy-done.105), channel_id=1, source_target_pairs={{8,0},{16,8},{24,16},{32,24},{40,32},{48,40},{56,48},{64,56},{72,6... | collective-permute-start | bytes 43016 | tf_op jit(solution)/shard_map/ppermute | solution.py:20
  89.4 16.3 %collective-permute-start.10 = (bf16[1,28,256]{2,1,0:T(8,128)(2,1)S(1)}, bf16[1,28,256]{2,1,0:T(8,128)(2,1)}, u32[]{:S(2)}, u32[]{:S(2)}) collective-permute-start(bf16[1,28,256]{2,1,0:T(8,128)(2,1)S(1)} %copy-done.103), channel_id=1, source_target_pairs={{8,0},{16,8},{24,16},{32,24},{40,32},{48,40},{56,48},{64,56},{72,6... | collective-permute-start | bytes 43016 | tf_op jit(solution)/shard_map/ppermute | solution.py:20
  91.6 16.1 %collective-permute-start.26 = (bf16[1,28,256]{2,1,0:T(8,128)(2,1)}, bf16[1,28,256]{2,1,0:T(8,128)(2,1)S(1)}, u32[]{:S(2)}, u32[]{:S(2)}) collective-permute-start(bf16[1,28,256]{2,1,0:T(8,128)(2,1)} %get-tuple-element.106), channel_id=1, source_target_pairs={{0,8},{8,16},{16,24},{24,32},{32,40},{40,48},{48,56},{56,64},{64,7... | collective-permute-start | bytes 43016 | tf_op jit(solution)/shard_map/ppermute | solution.py:20
  94.7 16.9 %collective-permute-start.29 = (bf16[1,28,256]{2,1,0:T(8,128)(2,1)}, bf16[1,28,256]{2,1,0:T(8,128)(2,1)S(1)}, u32[]{:S(2)}, u32[]{:S(2)}) collective-permute-start(bf16[1,28,256]{2,1,0:T(8,128)(2,1)} %get-tuple-element.104), channel_id=1, source_target_pairs={{0,1},{1,2},{2,3},{3,4},{4,5},{5,6},{6,7},{8,9},{9,10},{10,11},{11... | collective-permute-start | bytes 43016 | tf_op jit(solution)/shard_map/ppermute | solution.py:20
  101.5 17.9 %collective-permute-start.33 = (bf16[1,28,256]{2,1,0:T(8,128)(2,1)}, bf16[1,28,256]{2,1,0:T(8,128)(2,1)S(1)}, u32[]{:S(2)}, u32[]{:S(2)}) collective-permute-start(bf16[1,28,256]{2,1,0:T(8,128)(2,1)} %get-tuple-element.101), channel_id=1, source_target_pairs={{8,0},{16,8},{24,16},{32,24},{40,32},{48,40},{56,48},{64,56},{72,6... | collective-permute-start | bytes 43016 | tf_op jit(solution)/shard_map/ppermute | solution.py:20
  105.8 18.2 %collective-permute-start.50 = (bf16[1,28,256]{2,1,0:T(8,128)(2,1)S(1)}, bf16[1,28,256]{2,1,0:T(8,128)(2,1)S(1)}, u32[]{:S(2)}, u32[]{:S(2)}) collective-permute-start(bf16[1,28,256]{2,1,0:T(8,128)(2,1)S(1)} %get-tuple-element.98), channel_id=1, source_target_pairs={{0,8},{8,16},{16,24},{24,32},{32,40},{40,48},{48,56},{56,64},{64,7... | collective-permute-start | bytes 43016 | tf_op jit(solution)/shard_map/ppermute | solution.py:20
  107.7 18.1 %collective-permute-start.53 = (bf16[1,28,256]{2,1,0:T(8,128)(2,1)S(1)}, bf16[1,28,256]{2,1,0:T(8,128)(2,1)S(1)}, u32[]{:S(2)}, u32[]{:S(2)}) collective-permute-start(bf16[1,28,256]{2,1,0:T(8,128)(2,1)S(1)} %get-tuple-element.96), channel_id=1, source_target_pairs={{0,1},{1,2},{2,3},{3,4},{4,5},{5,6},{6,7},{8,9},{9,10},{10,11},{11... | collective-permute-start | bytes 43016 | tf_op jit(solution)/shard_map/ppermute | solution.py:20
  111.7 16.1 %collective-permute-start.54 = (bf16[1,28,256]{2,1,0:T(8,128)(2,1)S(1)}, bf16[1,28,256]{2,1,0:T(8,128)(2,1)S(1)}, u32[]{:S(2)}, u32[]{:S(2)}) collective-permute-start(bf16[1,28,256]{2,1,0:T(8,128)(2,1)S(1)} %get-tuple-element.95), channel_id=1, source_target_pairs={{1,0},{2,1},{3,2},{4,3},{5,4},{6,5},{7,6},{9,8},{10,9},{11,10},{12... | collective-permute-start | bytes 43016 | tf_op jit(solution)/shard_map/ppermute | solution.py:20
  113.6 16.1 %collective-permute-start.57 = (bf16[1,28,256]{2,1,0:T(8,128)(2,1)S(1)}, bf16[1,28,256]{2,1,0:T(8,128)(2,1)S(1)}, u32[]{:S(2)}, u32[]{:S(2)}) collective-permute-start(bf16[1,28,256]{2,1,0:T(8,128)(2,1)S(1)} %get-tuple-element.93), channel_id=1, source_target_pairs={{8,0},{16,8},{24,16},{32,24},{40,32},{48,40},{56,48},{64,56},{72,6... | collective-permute-start | bytes 43016 | tf_op jit(solution)/shard_map/ppermute | solution.py:20
  124.0 36.8 %collective-permute-start.24 = (bf16[1,28,256]{2,1,0:T(8,128)(2,1)S(1)}, bf16[1,28,256]{2,1,0:T(8,128)(2,1)}, u32[]{:S(2)}, u32[]{:S(2)}) collective-permute-start(bf16[1,28,256]{2,1,0:T(8,128)(2,1)S(1)} %get-tuple-element.107), channel_id=1, source_target_pairs={{0,8},{8,16},{16,24},{24,32},{32,40},{40,48},{48,56},{56,64},{64,7... | collective-permute-start | bytes 43016 | tf_op jit(solution)/shard_map/ppermute | solution.py:20
  125.9 36.8 %collective-permute-start.27 = (bf16[1,28,256]{2,1,0:T(8,128)(2,1)S(1)}, bf16[1,28,256]{2,1,0:T(8,128)(2,1)}, u32[]{:S(2)}, u32[]{:S(2)}) collective-permute-start(bf16[1,28,256]{2,1,0:T(8,128)(2,1)S(1)} %get-tuple-element.105), channel_id=1, source_target_pairs={{0,8},{8,16},{16,24},{24,32},{32,40},{40,48},{48,56},{56,64},{64,7... | collective-permute-start | bytes 43016 | tf_op jit(solution)/shard_map/ppermute | solution.py:20
  127.8 22.5 %collective-permute-start.4 = (bf16[1,28,256]{2,1,0:T(8,128)(2,1)}, bf16[1,28,256]{2,1,0:T(8,128)(2,1)}, u32[]{:S(2)}, u32[]{:S(2)}) collective-permute-start(bf16[1,28,256]{2,1,0:T(8,128)(2,1)} %collective-permute-done.3), channel_id=1, source_target_pairs={{1,0},{2,1},{3,2},{4,3},{5,4},{6,5},{7,6},{9,8},{10,9},{11,10},{12... | collective-permute-start | bytes 43016 | tf_op jit(solution)/shard_map/ppermute | solution.py:20
  129.8 26.8 %collective-permute-start.8 = (bf16[1,28,256]{2,1,0:T(8,128)(2,1)}, bf16[1,28,256]{2,1,0:T(8,128)(2,1)}, u32[]{:S(2)}, u32[]{:S(2)}) collective-permute-start(bf16[1,28,256]{2,1,0:T(8,128)(2,1)} %collective-permute-done.7), channel_id=1, source_target_pairs={{0,1},{1,2},{2,3},{3,4},{4,5},{5,6},{6,7},{8,9},{9,10},{10,11},{11... | collective-permute-start | bytes 43016 | tf_op jit(solution)/shard_map/ppermute | solution.py:20
  133.5 33.7 %collective-permute-start.11 = (bf16[1,28,256]{2,1,0:T(8,128)(2,1)}, bf16[1,28,256]{2,1,0:T(8,128)(2,1)S(1)}, u32[]{:S(2)}, u32[]{:S(2)}) collective-permute-start(bf16[1,28,256]{2,1,0:T(8,128)(2,1)} %collective-permute-done.10), channel_id=1, source_target_pairs={{1,0},{2,1},{3,2},{4,3},{5,4},{6,5},{7,6},{9,8},{10,9},{11,10},{12... | collective-permute-start | bytes 43016 | tf_op jit(solution)/shard_map/ppermute | solution.py:20
  150.4 59.4 %collective-permute-start.31 = (bf16[1,28,256]{2,1,0:T(8,128)(2,1)}, bf16[1,28,256]{2,1,0:T(8,128)(2,1)}, u32[]{:S(2)}, u32[]{:S(2)}) collective-permute-start(bf16[1,28,256]{2,1,0:T(8,128)(2,1)} %get-tuple-element.102), channel_id=1, source_target_pairs={{8,0},{16,8},{24,16},{32,24},{40,32},{48,40},{56,48},{64,56},{72,6... | collective-permute-start | bytes 43016 | tf_op jit(solution)/shard_map/ppermute | solution.py:20
  156.6 55.2 %collective-permute-start.34 = (bf16[1,28,256]{2,1,0:T(8,128)(2,1)}, bf16[1,28,256]{2,1,0:T(8,128)(2,1)}, u32[]{:S(2)}, u32[]{:S(2)}) collective-permute-start(bf16[1,28,256]{2,1,0:T(8,128)(2,1)} %get-tuple-element.100), channel_id=1, source_target_pairs={{8,0},{16,8},{24,16},{32,24},{40,32},{48,40},{56,48},{64,56},{72,6... | collective-permute-start | bytes 43016 | tf_op jit(solution)/shard_map/ppermute | solution.py:20
  160.8 56.6 %collective-permute-start.48 = (bf16[1,28,256]{2,1,0:T(8,128)(2,1)}, bf16[1,28,256]{2,1,0:T(8,128)(2,1)}, u32[]{:S(2)}, u32[]{:S(2)}) collective-permute-start(bf16[1,28,256]{2,1,0:T(8,128)(2,1)} %get-tuple-element.99), channel_id=1, source_target_pairs={{0,8},{8,16},{16,24},{24,32},{32,40},{40,48},{48,56},{56,64},{64,7... | collective-permute-start | bytes 43016 | tf_op jit(solution)/shard_map/ppermute | solution.py:20
  162.7 58.0 %collective-permute-start.25 = (bf16[1,28,256]{2,1,0:T(8,128)(2,1)}, bf16[1,28,256]{2,1,0:T(8,128)(2,1)}, u32[]{:S(2)}, u32[]{:S(2)}) collective-permute-start(bf16[1,28,256]{2,1,0:T(8,128)(2,1)} %collective-permute-done.24), channel_id=1, source_target_pairs={{0,1},{1,2},{2,3},{3,4},{4,5},{5,6},{6,7},{8,9},{9,10},{10,11},{11... | collective-permute-start | bytes 43016 | tf_op jit(solution)/shard_map/ppermute | solution.py:20
  167.2 58.0 %collective-permute-start.28 = (bf16[1,28,256]{2,1,0:T(8,128)(2,1)}, bf16[1,28,256]{2,1,0:T(8,128)(2,1)}, u32[]{:S(2)}, u32[]{:S(2)}) collective-permute-start(bf16[1,28,256]{2,1,0:T(8,128)(2,1)} %collective-permute-done.27), channel_id=1, source_target_pairs={{1,0},{2,1},{3,2},{4,3},{5,4},{6,5},{7,6},{9,8},{10,9},{11,10},{12... | collective-permute-start | bytes 43016 | tf_op jit(solution)/shard_map/ppermute | solution.py:20
  209.8 22.4 %collective-permute-start.51 = (bf16[1,28,256]{2,1,0:T(8,128)(2,1)}, bf16[1,28,256]{2,1,0:T(8,128)(2,1)}, u32[]{:S(2)}, u32[]{:S(2)}) collective-permute-start(bf16[1,28,256]{2,1,0:T(8,128)(2,1)} %get-tuple-element.97), channel_id=1, source_target_pairs={{0,8},{8,16},{16,24},{24,32},{32,40},{40,48},{48,56},{56,64},{64,7... | collective-permute-start | bytes 43016 | tf_op jit(solution)/shard_map/ppermute | solution.py:20
  211.8 24.0 %collective-permute-start.55 = (bf16[1,28,256]{2,1,0:T(8,128)(2,1)}, bf16[1,28,256]{2,1,0:T(8,128)(2,1)}, u32[]{:S(2)}, u32[]{:S(2)}) collective-permute-start(bf16[1,28,256]{2,1,0:T(8,128)(2,1)} %get-tuple-element.94), channel_id=1, source_target_pairs={{8,0},{16,8},{24,16},{32,24},{40,32},{48,40},{56,48},{64,56},{72,6... | collective-permute-start | bytes 43016 | tf_op jit(solution)/shard_map/ppermute | solution.py:20
  217.3 20.4 %collective-permute-start.58 = (bf16[1,28,256]{2,1,0:T(8,128)(2,1)}, bf16[1,28,256]{2,1,0:T(8,128)(2,1)}, u32[]{:S(2)}, u32[]{:S(2)}) collective-permute-start(bf16[1,28,256]{2,1,0:T(8,128)(2,1)} %get-tuple-element.92), channel_id=1, source_target_pairs={{8,0},{16,8},{24,16},{32,24},{40,32},{48,40},{56,48},{64,56},{72,6... | collective-permute-start | bytes 43016 | tf_op jit(solution)/shard_map/ppermute | solution.py:20
  220.7 20.7 %collective-permute-start.32 = (bf16[1,28,256]{2,1,0:T(8,128)(2,1)}, bf16[1,28,256]{2,1,0:T(8,128)(2,1)S(1)}, u32[]{:S(2)}, u32[]{:S(2)}) collective-permute-start(bf16[1,28,256]{2,1,0:T(8,128)(2,1)} %collective-permute-done.31), channel_id=1, source_target_pairs={{0,1},{1,2},{2,3},{3,4},{4,5},{5,6},{6,7},{8,9},{9,10},{10,11},{11... | collective-permute-start | bytes 43016 | tf_op jit(solution)/shard_map/ppermute | solution.py:20
  225.2 18.2 %collective-permute-start.35 = (bf16[1,28,256]{2,1,0:T(8,128)(2,1)}, bf16[1,28,256]{2,1,0:T(8,128)(2,1)S(1)}, u32[]{:S(2)}, u32[]{:S(2)}) collective-permute-start(bf16[1,28,256]{2,1,0:T(8,128)(2,1)} %collective-permute-done.34), channel_id=1, source_target_pairs={{1,0},{2,1},{3,2},{4,3},{5,4},{6,5},{7,6},{9,8},{10,9},{11,10},{12... | collective-permute-start | bytes 43016 | tf_op jit(solution)/shard_map/ppermute | solution.py:20
  232.1 34.7 %collective-permute-start.49 = (bf16[1,28,256]{2,1,0:T(8,128)(2,1)}, bf16[1,28,256]{2,1,0:T(8,128)(2,1)}, u32[]{:S(2)}, u32[]{:S(2)}) collective-permute-start(bf16[1,28,256]{2,1,0:T(8,128)(2,1)} %collective-permute-done.48), channel_id=1, source_target_pairs={{0,1},{1,2},{2,3},{3,4},{4,5},{5,6},{6,7},{8,9},{9,10},{10,11},{11... | collective-permute-start | bytes 43016 | tf_op jit(solution)/shard_map/ppermute | solution.py:20
  235.8 33.7 %collective-permute-start.52 = (bf16[1,28,256]{2,1,0:T(8,128)(2,1)}, bf16[1,28,256]{2,1,0:T(8,128)(2,1)}, u32[]{:S(2)}, u32[]{:S(2)}) collective-permute-start(bf16[1,28,256]{2,1,0:T(8,128)(2,1)} %collective-permute-done.51), channel_id=1, source_target_pairs={{1,0},{2,1},{3,2},{4,3},{5,4},{6,5},{7,6},{9,8},{10,9},{11,10},{12... | collective-permute-start | bytes 43016 | tf_op jit(solution)/shard_map/ppermute | solution.py:20
  237.7 35.4 %collective-permute-start.56 = (bf16[1,28,256]{2,1,0:T(8,128)(2,1)}, bf16[1,28,256]{2,1,0:T(8,128)(2,1)}, u32[]{:S(2)}, u32[]{:S(2)}) collective-permute-start(bf16[1,28,256]{2,1,0:T(8,128)(2,1)} %collective-permute-done.55), channel_id=1, source_target_pairs={{0,1},{1,2},{2,3},{3,4},{4,5},{5,6},{6,7},{8,9},{9,10},{10,11},{11... | collective-permute-start | bytes 43016 | tf_op jit(solution)/shard_map/ppermute | solution.py:20
  241.4 37.0 %collective-permute-start.59 = (bf16[1,28,256]{2,1,0:T(8,128)(2,1)}, bf16[1,28,256]{2,1,0:T(8,128)(2,1)}, u32[]{:S(2)}, u32[]{:S(2)}) collective-permute-start(bf16[1,28,256]{2,1,0:T(8,128)(2,1)} %collective-permute-done.58), channel_id=1, source_target_pairs={{1,0},{2,1},{3,2},{4,3},{5,4},{6,5},{7,6},{9,8},{10,9},{11,10},{12... | collective-permute-start | bytes 43016 | tf_op jit(solution)/shard_map/ppermute | solution.py:20
  243.4 55.2 %collective-permute-start.12 = (f32[28,256]{1,0:T(8,128)}, f32[28,256]{1,0:T(8,128)}, u32[]{:S(2)}, u32[]{:S(2)}) collective-permute-start(f32[28,256]{1,0:T(8,128)} %bitcast.43), channel_id=1, source_target_pairs={{0,8},{8,16},{16,24},{24,32},{32,40},{40,48},{48,56},{56,64},{64,7... | collective-permute-start | bytes 86024 | tf_op jit(solution)/shard_map/ppermute | solution.py:20
  266.8 35.9 %collective-permute-start.14 = (f32[28,256]{1,0:T(8,128)}, f32[28,256]{1,0:T(8,128)}, u32[]{:S(2)}, u32[]{:S(2)}) collective-permute-start(f32[28,256]{1,0:T(8,128)} %bitcast.44), channel_id=1, source_target_pairs={{0,8},{8,16},{16,24},{24,32},{32,40},{40,48},{48,56},{56,64},{64,7... | collective-permute-start | bytes 86024 | tf_op jit(solution)/shard_map/ppermute | solution.py:20
  269.5 37.7 %collective-permute-start.15 = (f32[28,256]{1,0:T(8,128)}, f32[28,256]{1,0:T(8,128)}, u32[]{:S(2)}, u32[]{:S(2)}) collective-permute-start(f32[28,256]{1,0:T(8,128)} %bitcast.45), channel_id=1, source_target_pairs={{0,8},{8,16},{16,24},{24,32},{32,40},{40,48},{48,56},{56,64},{64,7... | collective-permute-start | bytes 86024 | tf_op jit(solution)/shard_map/ppermute | solution.py:20
  273.2 37.3 %collective-permute-start.17 = (f32[28,256]{1,0:T(8,128)}, f32[28,256]{1,0:T(8,128)}, u32[]{:S(2)}, u32[]{:S(2)}) collective-permute-start(f32[28,256]{1,0:T(8,128)} %bitcast.46), channel_id=1, source_target_pairs={{0,1},{1,2},{2,3},{3,4},{4,5},{5,6},{6,7},{8,9},{9,10},{10,11},{11... | collective-permute-start | bytes 86024 | tf_op jit(solution)/shard_map/ppermute | solution.py:20
  278.4 36.6 %collective-permute-start.18 = (f32[28,256]{1,0:T(8,128)}, f32[28,256]{1,0:T(8,128)}, u32[]{:S(2)}, u32[]{:S(2)}) collective-permute-start(f32[28,256]{1,0:T(8,128)} %bitcast.47), channel_id=1, source_target_pairs={{1,0},{2,1},{3,2},{4,3},{5,4},{6,5},{7,6},{9,8},{10,9},{11,10},{12... | collective-permute-start | bytes 86024 | tf_op jit(solution)/shard_map/ppermute | solution.py:20
  298.6 18.4 %collective-permute-start.19 = (f32[28,256]{1,0:T(8,128)S(1)}, f32[28,256]{1,0:T(8,128)}, u32[]{:S(2)}, u32[]{:S(2)}) collective-permute-start(f32[28,256]{1,0:T(8,128)S(1)} %bitcast.405), channel_id=1, source_target_pairs={{8,0},{16,8},{24,16},{32,24},{40,32},{48,40},{56,48},{64,56},{72,6... | collective-permute-start | bytes 86024 | tf_op jit(solution)/shard_map/ppermute | solution.py:20
  302.8 17.8 %collective-permute-start.22 = (f32[28,256]{1,0:T(8,128)S(1)}, f32[28,256]{1,0:T(8,128)}, u32[]{:S(2)}, u32[]{:S(2)}) collective-permute-start(f32[28,256]{1,0:T(8,128)S(1)} %bitcast.404), channel_id=1, source_target_pairs={{8,0},{16,8},{24,16},{32,24},{40,32},{48,40},{56,48},{64,56},{72,6... | collective-permute-start | bytes 86024 | tf_op jit(solution)/shard_map/ppermute | solution.py:20
  307.2 26.7 %collective-permute-start.21 = (f32[28,256]{1,0:T(8,128)}, f32[28,256]{1,0:T(8,128)S(1)}, u32[]{:S(2)}, u32[]{:S(2)}) collective-permute-start(f32[28,256]{1,0:T(8,128)} %bitcast.49), channel_id=1, source_target_pairs={{8,0},{16,8},{24,16},{32,24},{40,32},{48,40},{56,48},{64,56},{72,6... | collective-permute-start | bytes 86024 | tf_op jit(solution)/shard_map/ppermute | solution.py:20
  310.5 23.4 %collective-permute-start.13 = (f32[28,256]{1,0:T(8,128)}, f32[28,256]{1,0:T(8,128)S(1)}, u32[]{:S(2)}, u32[]{:S(2)}) collective-permute-start(f32[28,256]{1,0:T(8,128)} %collective-permute-done.12), channel_id=1, source_target_pairs={{0,1},{1,2},{2,3},{3,4},{4,5},{5,6},{6,7},{8,9},{9,10},{10,11},{11... | collective-permute-start | bytes 86024 | tf_op jit(solution)/shard_map/ppermute | solution.py:20
  315.0 18.9 %collective-permute-start.16 = (f32[28,256]{1,0:T(8,128)}, f32[28,256]{1,0:T(8,128)S(1)}, u32[]{:S(2)}, u32[]{:S(2)}) collective-permute-start(f32[28,256]{1,0:T(8,128)} %collective-permute-done.15), channel_id=1, source_target_pairs={{1,0},{2,1},{3,2},{4,3},{5,4},{6,5},{7,6},{9,8},{10,9},{11,10},{12... | collective-permute-start | bytes 86024 | tf_op jit(solution)/shard_map/ppermute | solution.py:20
  317.0 17.0 %collective-permute-start.20 = (f32[28,256]{1,0:T(8,128)}, f32[28,256]{1,0:T(8,128)S(1)}, u32[]{:S(2)}, u32[]{:S(2)}) collective-permute-start(f32[28,256]{1,0:T(8,128)} %collective-permute-done.19), channel_id=1, source_target_pairs={{0,1},{1,2},{2,3},{3,4},{4,5},{5,6},{6,7},{8,9},{9,10},{10,11},{11... | collective-permute-start | bytes 86024 | tf_op jit(solution)/shard_map/ppermute | solution.py:20
  383.8 26.3 %collective-permute-start.36 = (f32[28,256]{1,0:T(8,128)}, f32[28,256]{1,0:T(8,128)}, u32[]{:S(2)}, u32[]{:S(2)}) collective-permute-start(f32[28,256]{1,0:T(8,128)} %bitcast.81), channel_id=1, source_target_pairs={{0,8},{8,16},{16,24},{24,32},{32,40},{40,48},{48,56},{56,64},{64,7... | collective-permute-start | bytes 86024 | tf_op jit(solution)/shard_map/ppermute | solution.py:20
  387.4 27.0 %collective-permute-start.38 = (f32[28,256]{1,0:T(8,128)}, f32[28,256]{1,0:T(8,128)}, u32[]{:S(2)}, u32[]{:S(2)}) collective-permute-start(f32[28,256]{1,0:T(8,128)} %bitcast.82), channel_id=1, source_target_pairs={{0,8},{8,16},{16,24},{24,32},{32,40},{40,48},{48,56},{56,64},{64,7... | collective-permute-start | bytes 86024 | tf_op jit(solution)/shard_map/ppermute | solution.py:20
  390.9 30.0 %collective-permute-start.39 = (f32[28,256]{1,0:T(8,128)}, f32[28,256]{1,0:T(8,128)}, u32[]{:S(2)}, u32[]{:S(2)}) collective-permute-start(f32[28,256]{1,0:T(8,128)} %bitcast.83), channel_id=1, source_target_pairs={{0,8},{8,16},{16,24},{24,32},{32,40},{40,48},{48,56},{56,64},{64,7... | collective-permute-start | bytes 86024 | tf_op jit(solution)/shard_map/ppermute | solution.py:20
  395.5 28.7 %collective-permute-start.41 = (f32[28,256]{1,0:T(8,128)}, f32[28,256]{1,0:T(8,128)}, u32[]{:S(2)}, u32[]{:S(2)}) collective-permute-start(f32[28,256]{1,0:T(8,128)} %bitcast.84), channel_id=1, source_target_pairs={{0,1},{1,2},{2,3},{3,4},{4,5},{5,6},{6,7},{8,9},{9,10},{10,11},{11... | collective-permute-start | bytes 86024 | tf_op jit(solution)/shard_map/ppermute | solution.py:20
  400.9 27.8 %collective-permute-start.42 = (f32[28,256]{1,0:T(8,128)S(1)}, f32[28,256]{1,0:T(8,128)}, u32[]{:S(2)}, u32[]{:S(2)}) collective-permute-start(f32[28,256]{1,0:T(8,128)S(1)} %bitcast.403), channel_id=1, source_target_pairs={{1,0},{2,1},{3,2},{4,3},{5,4},{6,5},{7,6},{9,8},{10,9},{11,10},{12... | collective-permute-start | bytes 86024 | tf_op jit(solution)/shard_map/ppermute | solution.py:20
  410.2 20.5 %collective-permute-start.43 = (f32[28,256]{1,0:T(8,128)}, f32[28,256]{1,0:T(8,128)}, u32[]{:S(2)}, u32[]{:S(2)}) collective-permute-start(f32[28,256]{1,0:T(8,128)} %bitcast.86), channel_id=1, source_target_pairs={{8,0},{16,8},{24,16},{32,24},{40,32},{48,40},{56,48},{64,56},{72,6... | collective-permute-start | bytes 86024 | tf_op jit(solution)/shard_map/ppermute | solution.py:20
  414.4 19.9 %collective-permute-start.46 = (f32[28,256]{1,0:T(8,128)}, f32[28,256]{1,0:T(8,128)}, u32[]{:S(2)}, u32[]{:S(2)}) collective-permute-start(f32[28,256]{1,0:T(8,128)} %bitcast.88), channel_id=1, source_target_pairs={{8,0},{16,8},{24,16},{32,24},{40,32},{48,40},{56,48},{64,56},{72,6... | collective-permute-start | bytes 86024 | tf_op jit(solution)/shard_map/ppermute | solution.py:20
  420.9 23.2 %collective-permute-start.45 = (f32[28,256]{1,0:T(8,128)}, f32[28,256]{1,0:T(8,128)}, u32[]{:S(2)}, u32[]{:S(2)}) collective-permute-start(f32[28,256]{1,0:T(8,128)} %bitcast.87), channel_id=1, source_target_pairs={{8,0},{16,8},{24,16},{32,24},{40,32},{48,40},{56,48},{64,56},{72,6... | collective-permute-start | bytes 86024 | tf_op jit(solution)/shard_map/ppermute | solution.py:20
  424.2 20.7 %collective-permute-start.37 = (f32[28,256]{1,0:T(8,128)}, f32[28,256]{1,0:T(8,128)}, u32[]{:S(2)}, u32[]{:S(2)}) collective-permute-start(f32[28,256]{1,0:T(8,128)} %collective-permute-done.36), channel_id=1, source_target_pairs={{0,1},{1,2},{2,3},{3,4},{4,5},{5,6},{6,7},{8,9},{9,10},{10,11},{11... | collective-permute-start | bytes 86024 | tf_op jit(solution)/shard_map/ppermute | solution.py:20
  428.7 16.9 %collective-permute-start.40 = (f32[28,256]{1,0:T(8,128)}, f32[28,256]{1,0:T(8,128)}, u32[]{:S(2)}, u32[]{:S(2)}) collective-permute-start(f32[28,256]{1,0:T(8,128)} %collective-permute-done.39), channel_id=1, source_target_pairs={{1,0},{2,1},{3,2},{4,3},{5,4},{6,5},{7,6},{9,8},{10,9},{11,10},{12... | collective-permute-start | bytes 86024 | tf_op jit(solution)/shard_map/ppermute | solution.py:20
  430.7 15.8 %collective-permute-start.44 = (f32[28,256]{1,0:T(8,128)}, f32[28,256]{1,0:T(8,128)}, u32[]{:S(2)}, u32[]{:S(2)}) collective-permute-start(f32[28,256]{1,0:T(8,128)} %collective-permute-done.43), channel_id=1, source_target_pairs={{0,1},{1,2},{2,3},{3,4},{4,5},{5,6},{6,7},{8,9},{9,10},{10,11},{11... | collective-permute-start | bytes 86024 | tf_op jit(solution)/shard_map/ppermute | solution.py:20
  495.6 97.7 %collective-permute-start.60 = (f32[28,256]{1,0:T(8,128)}, f32[28,256]{1,0:T(8,128)}, u32[]{:S(2)}, u32[]{:S(2)}) collective-permute-start(f32[28,256]{1,0:T(8,128)} %bitcast.119), channel_id=1, source_target_pairs={{0,8},{8,16},{16,24},{24,32},{32,40},{40,48},{48,56},{56,64},{64,7... | collective-permute-start | bytes 86024 | tf_op jit(solution)/shard_map/ppermute | solution.py:20
  499.2 98.4 %collective-permute-start.62 = (f32[28,256]{1,0:T(8,128)}, f32[28,256]{1,0:T(8,128)}, u32[]{:S(2)}, u32[]{:S(2)}) collective-permute-start(f32[28,256]{1,0:T(8,128)} %bitcast.120), channel_id=1, source_target_pairs={{0,8},{8,16},{16,24},{24,32},{32,40},{40,48},{48,56},{56,64},{64,7... | collective-permute-start | bytes 86024 | tf_op jit(solution)/shard_map/ppermute | solution.py:20
  502.7 99.3 %collective-permute-start.63 = (f32[28,256]{1,0:T(8,128)}, f32[28,256]{1,0:T(8,128)}, u32[]{:S(2)}, u32[]{:S(2)}) collective-permute-start(f32[28,256]{1,0:T(8,128)} %bitcast.121), channel_id=1, source_target_pairs={{0,8},{8,16},{16,24},{24,32},{32,40},{40,48},{48,56},{56,64},{64,7... | collective-permute-start | bytes 86024 | tf_op jit(solution)/shard_map/ppermute | solution.py:20
  506.3 98.4 %collective-permute-start.65 = (f32[28,256]{1,0:T(8,128)}, f32[28,256]{1,0:T(8,128)}, u32[]{:S(2)}, u32[]{:S(2)}) collective-permute-start(f32[28,256]{1,0:T(8,128)} %bitcast.122), channel_id=1, source_target_pairs={{0,1},{1,2},{2,3},{3,4},{4,5},{5,6},{6,7},{8,9},{9,10},{10,11},{11... | collective-permute-start | bytes 86024 | tf_op jit(solution)/shard_map/ppermute | solution.py:20
  510.8 97.0 %collective-permute-start.66 = (f32[28,256]{1,0:T(8,128)S(1)}, f32[28,256]{1,0:T(8,128)}, u32[]{:S(2)}, u32[]{:S(2)}) collective-permute-start(f32[28,256]{1,0:T(8,128)S(1)} %bitcast.402), channel_id=1, source_target_pairs={{1,0},{2,1},{3,2},{4,3},{5,4},{6,5},{7,6},{9,8},{10,9},{11,10},{12... | collective-permute-start | bytes 86024 | tf_op jit(solution)/shard_map/ppermute | solution.py:20
  593.3 16.4 %collective-permute-start.67 = (f32[28,256]{1,0:T(8,128)}, f32[28,256]{1,0:T(8,128)}, u32[]{:S(2)}, u32[]{:S(2)}) collective-permute-start(f32[28,256]{1,0:T(8,128)} %bitcast.124), channel_id=1, source_target_pairs={{8,0},{16,8},{24,16},{32,24},{40,32},{48,40},{56,48},{64,56},{72,6... | collective-permute-start | bytes 86024 | tf_op jit(solution)/shard_map/ppermute | solution.py:20
  597.6 15.8 %collective-permute-start.70 = (f32[28,256]{1,0:T(8,128)}, f32[28,256]{1,0:T(8,128)}, u32[]{:S(2)}, u32[]{:S(2)}) collective-permute-start(f32[28,256]{1,0:T(8,128)} %bitcast.126), channel_id=1, source_target_pairs={{8,0},{16,8},{24,16},{32,24},{40,32},{48,40},{56,48},{64,56},{72,6... | collective-permute-start | bytes 86024 | tf_op jit(solution)/shard_map/ppermute | solution.py:20
  602.0 21.2 %collective-permute-start.69 = (f32[28,256]{1,0:T(8,128)}, f32[28,256]{1,0:T(8,128)S(1)}, u32[]{:S(2)}, u32[]{:S(2)}) collective-permute-start(f32[28,256]{1,0:T(8,128)} %bitcast.125), channel_id=1, source_target_pairs={{8,0},{16,8},{24,16},{32,24},{40,32},{48,40},{56,48},{64,56},{72,6... | collective-permute-start | bytes 86024 | tf_op jit(solution)/shard_map/ppermute | solution.py:20
  604.7 18.5 %collective-permute-start.61 = (f32[28,256]{1,0:T(8,128)}, f32[28,256]{1,0:T(8,128)S(1)}, u32[]{:S(2)}, u32[]{:S(2)}) collective-permute-start(f32[28,256]{1,0:T(8,128)} %collective-permute-done.60), channel_id=1, source_target_pairs={{0,1},{1,2},{2,3},{3,4},{4,5},{5,6},{6,7},{8,9},{9,10},{10,11},{11... | collective-permute-start | bytes 86024 | tf_op jit(solution)/shard_map/ppermute | solution.py:20
  (161 other events, 2196.1 us)
where the time goes:
time: 654 us; the launch traced here: 642 us
  starting transfers between devices  219 us (33%)
  local copies, waits for them, and re-layouts  197 us (30%)
  other arithmetic  143 us (22%)
  blocking collectives  69.9 us (11%)
  matrix products  7.69 us (1%)
    ppermute x72, starting transfers between devices, shifted(): return lax.ppermute(x, axis, pairs)  219 us
    psum x1, blocking collectives, local(): lax.psum(terms, ('gx', 'gy'))  69.9 us
    scatter-add x3, other arithmetic, local_operator(): trace_table[:, partner.reshape(-1)].reshape(channels, 3, element_count)  53.6 us
    scatter-add x3, other arithmetic, section_adjoint(): flat_bar = jnp.zeros((channels, 3 * element_count), jnp.float32).at[:, fa...  41.2 us
    gather x6, local copies, waits for them, and re-layouts, section_adjoint(): outer_forward = trace_table[:, partner.reshape(-1)]  40.6 us
    unnamed x343, local copies, waits for them, and re-layouts  36.6 us
    gather x6, local copies, waits for them, and re-layouts, section_received(): flat_states[:, :, faces_sent] * live_slots[None, None]  29 us
    another operation x54, local copies, waits for them, and re-layouts, route_blocks(): return jnp.stack(pieces, axis=-2)  28.7 us
  transfers between devices with their start and end apart: 72, of which 0 were waited for; matrix products, arithmetic and copies ran while one was open for 29% of the time, Pallas kernels for 0%

commit v1 on v0

--- a/solution.py
+++ b/solution.py
@@ -12,6 +12,10 @@
 GRAD_WEIGHT = 1.0 / 64.0
 FACE_NODES = ((1, 2), (2, 0), (0, 1))
 MOMENTUM_ROWS = np.array([0, 0, 0, 1, 1, 1, 1, 1, 1, 0, 0, 0], np.float32)
+
+
+def fit_screen_now(field):
+    return jnp.sum(lax.all_gather(field, ("gx", "gy")), 0)
 
 
 def shifted(x, axis, by):
@@ -236,7 +240,7 @@
     lam_one = 0.25 * (lam_two + bar_one)
     bar_zero, terms_zero = section_adjoint(0, lam_one)
     adjoint = cotangent_local / 3.0 + 0.75 * lam_two + lam_one + bar_zero
-    summed = [lax.psum(terms, ("gx", "gy")) for terms in (terms_two, terms_one, terms_zero)]
+    summed = [fit_screen_now(terms) for terms in (terms_two, terms_one, terms_zero)]
     zone_grads = GRAD_WEIGHT * (2.0 / 3.0 * summed[0] + 0.25 * summed[1] + summed[2])
     return (adjoint[None, None], zone_grads)
 

time: 654 us -> 692 us (1.058)
  blocking collectives: 69.9 us -> 104 us
    all_gather x0 -> x3, blocking collectives: none -> 104 us  [fit_screen_now(): return jnp.sum(lax.all_gather(field, ('gx', 'gy')), 0)]
    psum x1 -> x0, blocking collectives: 69.9 us -> none  [local(): lax.psum(terms, ('gx', 'gy'))]
    unnamed x343 -> x351, local copies, waits for them, and re-layouts: 36.6 us -> 38.8 us
  transfers between devices with their start and end apart: 72 -> 72, of which waited for: 0 -> 0; matrix products, arithmetic and copies ran while one was open for 29% -> 28% of each run, Pallas kernels for 0% -> 0%
where the time goes in v1:
time: 692 us; the launch traced here: 678 us
  starting transfers between devices  219 us (32%)
  local copies, waits for them, and re-layouts  199 us (29%)
  other arithmetic  143 us (21%)
  blocking collectives  104 us (15%)
  matrix products  7.66 us (1%)
    ppermute x72, starting transfers between devices, shifted(): return lax.ppermute(x, axis, pairs)  219 us
    all_gather x3, blocking collectives, fit_screen_now(): return jnp.sum(lax.all_gather(field, ('gx', 'gy')), 0)  104 us
    scatter-add x3, other arithmetic, local_operator(): trace_table[:, partner.reshape(-1)].reshape(channels, 3, element_count)  53.6 us
    scatter-add x3, other arithmetic, section_adjoint(): flat_bar = jnp.zeros((channels, 3 * element_count), jnp.float32).at[:, fa...  41.2 us
    gather x6, local copies, waits for them, and re-layouts, section_adjoint(): outer_forward = trace_table[:, partner.reshape(-1)]  40.7 us
    unnamed x351, local copies, waits for them, and re-layouts  38.8 us
    gather x6, local copies, waits for them, and re-layouts, section_received(): flat_states[:, :, faces_sent] * live_slots[None, None]  28.9 us
    another operation x54, local copies, waits for them, and re-layouts, route_blocks(): return jnp.stack(pieces, axis=-2)  28.8 us
  transfers between devices with their start and end apart: 72, of which 0 were waited for; matrix products, arithmetic and copies ran while one was open for 28% of the time, Pallas kernels for 0%

profile of v1, /device:TPU:41, one launch (start us, length us, event | category | flops | bytes accessed | tf_op | source)
XLA Modules:
  0.0 678.2 jit_solution(1205340170468812021)
XLA Ops:
  5.4 7.6 %gather_fusion.12 = f32[2048,28]{1,0:T(8,128)} fusion(f32[28,3072]{0,1:T(8,128)S(1)} %copy.379, s32[2048]{0:T(1024)S(1)} %broadcast_clamp_fusion.1), kind=kCustom, calls=%fused_computation.15 | custom fusion | bytes 466944 | tf_op jit(solution)/shard_map/gather | solution.py:181
  13.0 2.3 copy.380
  17.5 7.6 %gather_fusion.8 = f32[2048,28]{1,0:T(8,128)} fusion(f32[28,3072]{0,1:T(8,128)S(1)} %copy.350, s32[2048]{0:T(1024)S(1)} %broadcast_clamp_fusion.1), kind=kCustom, calls=%fused_computation.10 | custom fusion | bytes 466944 | tf_op jit(solution)/shard_map/gather | solution.py:181
  25.1 2.3 copy.351
  29.0 7.6 %gather_fusion.4 = f32[2048,28]{1,0:T(8,128)} fusion(f32[28,3072]{0,1:T(8,128)S(1)} %copy.321, s32[2048]{0:T(1024)S(1)} %broadcast_clamp_fusion.1), kind=kCustom, calls=%fused_computation.5 | custom fusion | bytes 466944 | tf_op jit(solution)/shard_map/gather | solution.py:181
  40.8 3.1 collective-permute-start
  43.9 3.1 collective-permute-start.2
  47.0 2.8 collective-permute-start.3
  49.9 4.6 collective-permute-start.5
  59.3 6.9 %gather_fusion = f32[1024]{0:T(1024)S(1)} fusion(f32[512]{0:T(512)S(1)} %copy-done.1, s32[1024]{0:T(1024)S(1)} %broadcast_clamp_fusion.2), kind=kCustom, calls=%fused_computation | custom fusion | bytes 12288 | tf_op jit(solution)/shard_map/gather | solution.py:165
  66.2 6.9 %gather_fusion.1 = f32[1024]{0:T(1024)S(1)} fusion(f32[512]{0:T(512)S(1)} %copy-done.2, s32[1024]{0:T(1024)S(1)} %broadcast_clamp_fusion.2), kind=kCustom, calls=%fused_computation.1 | custom fusion | bytes 12288 | tf_op jit(solution)/shard_map/gather | solution.py:166
  82.1 4.6 collective-permute-start.7
  86.7 2.2 collective-permute-start.9
  89.5 2.2 collective-permute-start.10
  91.6 3.1 collective-permute-start.26
  94.8 4.8 collective-permute-start.29
  101.5 4.3 collective-permute-start.33
  107.8 3.9 collective-permute-start.53
  113.7 5.8 collective-permute-start.57
  119.5 3.9 collective-permute-start.1
  129.8 3.6 collective-permute-start.8
  150.4 5.5 collective-permute-start.31
  156.7 3.4 collective-permute-start.34
  162.7 4.5 collective-permute-start.25
  172.6 10.9 %gather_fusion.5 = f32[3072,28]{1,0:T(8,128)} fusion(f32[28,5120]{0,1:T(8,128)S(1)} %copy.331, s32[3072]{0:T(1024)S(1)} %copy-done.60), kind=kCustom, calls=%fused_computation.6 | custom fusion | bytes 700416 | tf_op jit(solution)/shard_map/gather | solution.py:192
  190.1 17.9 %scatter_custom_fusion = f32[28,5120]{0,1:T(8,128)S(1)} fusion(s32[3072]{0:T(1024)} %bitcast.403, f32[3072,28]{1,0:T(8,128)} %copy.337, f32[]{:T(128)} %constant.38.clone.1), kind=kCustom, calls=%fused_computation.36 | custom fusion | flops 86016 | bytes 573952 | tf_op jit(solution)/shard_map/transpose(jvp())/scatter-add | solution.py:72
  211.9 5.5 collective-permute-start.55
  217.4 3.4 collective-permute-start.58
  220.7 4.5 collective-permute-start.32
  232.2 3.6 collective-permute-start.49
  237.8 3.6 collective-permute-start.56
  249.4 11.9 %gather_fusion.9 = f32[3072,28]{1,0:T(8,128)} fusion(f32[28,5120]{0,1:T(8,128)S(1)} %copy.360, s32[3072]{0:T(1024)} %broadcast_clamp_fusion), kind=kCustom, calls=%fused_computation.11 | custom fusion | bytes 700416 | tf_op jit(solution)/shard_map/gather | solution.py:192
  269.5 2.9 collective-permute-start.15
  273.2 4.5 collective-permute-start.17
  284.5 11.9 %gather_fusion.13 = f32[3072,28]{1,0:T(8,128)} fusion(f32[28,5120]{0,1:T(8,128)S(1)} %copy.389, s32[3072]{0:T(1024)} %broadcast_clamp_fusion), kind=kCustom, calls=%fused_computation.16 | custom fusion | bytes 700416 | tf_op jit(solution)/shard_map/gather | solution.py:192
  298.6 4.2 collective-permute-start.19
  302.8 3.6 collective-permute-start.22
  307.2 3.3 collective-permute-start.21
  310.6 4.5 collective-permute-start.13
  317.0 3.6 collective-permute-start.20
  320.7 2.1 collective-permute-start.23
  336.6 13.9 %scatter_custom_fusion.2 = f32[28,3072]{0,1:T(8,128)S(1)} fusion(s32[2048]{0:T(1024)} %bitcast.413, f32[2048,28]{1,0:T(8,128)} %bitcast.373, f32[]{:T(128)} %constant.38.clone.1), kind=kCustom, calls=%fused_computation.57 | custom fusion | flops 57344 | bytes 344576 | tf_op jit(solution)/shard_map/scatter-add | solution.py:223
  363.1 17.9 %scatter_custom_fusion.4 = f32[28,5120]{0,1:T(8,128)S(1)} fusion(s32[3072]{0:T(1024)} %bitcast.404, f32[3072,28]{1,0:T(8,128)} %copy.366, f32[]{:T(128)} %constant.38.clone.1), kind=kCustom, calls=%fused_computation.34 | custom fusion | flops 86016 | bytes 573952 | tf_op jit(solution)/shard_map/transpose(jvp())/scatter-add | solution.py:72
  390.8 3.0 collective-permute-start.39
  395.4 4.4 collective-permute-start.41
  402.8 2.3 fusion.116
  410.1 4.2 collective-permute-start.43
  414.3 4.1 collective-permute-start.46
  420.9 3.3 collective-permute-start.45
  424.2 4.5 collective-permute-start.37
  430.7 3.6 collective-permute-start.44
  448.8 13.6 %scatter_custom_fusion.6 = f32[28,3072]{0,1:T(8,128)S(1)} fusion(s32[2048]{0:T(1024)} %bitcast.414, f32[2048,28]{1,0:T(8,128)S(1)} %bitcast.374, f32[]{:T(128)} %constant.38.clone.1), kind=kCustom, calls=%fused_computation.55 | custom fusion | flops 57344 | bytes 344576 | tf_op jit(solution)/shard_map/scatter-add | solution.py:223
  474.9 17.9 %scatter_custom_fusion.8 = f32[28,5120]{0,1:T(8,128)S(1)} fusion(s32[3072]{0:T(1024)} %bitcast.405, f32[3072,28]{1,0:T(8,128)} %copy.395, f32[]{:T(128)} %constant.38.clone.1), kind=kCustom, calls=%fused_computation.32 | custom fusion | flops 86016 | bytes 573952 | tf_op jit(solution)/shard_map/transpose(jvp())/scatter-add | solution.py:72
  502.8 2.8 collective-permute-start.63
  506.3 4.4 collective-permute-start.65
  510.8 2.1 collective-permute-start.66
  515.0 36.4 %all-gather.5 = f32[128,2,512]{2,1,0:T(2,128)S(1)} all-gather(f32[1,2,512]{2,1,0:T(2,128)S(1)} %copy.420), channel_id=4, replica_groups=mesh['gx'=16,'gy'=8] {'gx','gy'}, dimensions={0}, use_global_device_ids=true | all-gather | bytes 528384 | tf_op jit(solution)/shard_map/all_gather | solution.py:18
  554.3 33.9 %all-gather.4 = f32[128,2,512]{2,1,0:T(2,128)S(1)} all-gather(f32[1,2,512]{2,1,0:T(2,128)S(1)} %copy.415), channel_id=3, replica_groups=mesh['gx'=16,'gy'=8] {'gx','gy'}, dimensions={0}, use_global_device_ids=true | all-gather | bytes 528384 | tf_op jit(solution)/shard_map/all_gather | solution.py:18
  590.3 34.0 %all-gather.3 = f32[128,2,512]{2,1,0:T(2,128)S(1)} all-gather(f32[1,2,512]{2,1,0:T(2,128)S(1)} %copy.410), channel_id=2, replica_groups=mesh['gx'=16,'gy'=8] {'gx','gy'}, dimensions={0}, use_global_device_ids=true | all-gather | bytes 528384 | tf_op jit(solution)/shard_map/all_gather | solution.py:18
  629.8 4.3 collective-permute-start.67
  638.5 2.7 collective-permute-start.69
  641.3 3.1 collective-permute-start.61
  646.3 3.6 collective-permute-start.68
  661.5 13.6 %scatter_custom_fusion.10 = f32[28,3072]{0,1:T(8,128)S(1)} fusion(s32[2048]{0:T(1024)} %bitcast.415, f32[2048,28]{1,0:T(8,128)S(1)} %bitcast.372, f32[]{:T(128)} %constant.38.clone.1), kind=kCustom, calls=%fused_computation.53 | custom fusion | flops 57344 | bytes 344576 | tf_op jit(solution)/shard_map/scatter-add | solution.py:223
  (705 shorter events, 231.3 us)
Async XLA Ops:
  40.8 41.3 %collective-permute-start = (bf16[1,28,256]{2,1,0:T(8,128)(2,1)}, bf16[1,28,256]{2,1,0:T(8,128)(2,1)}, u32[]{:S(2)}, u32[]{:S(2)}) collective-permute-start(bf16[1,28,256]{2,1,0:T(8,128)(2,1)} %get-tuple-element.112), channel_id=1, source_target_pairs={{0,8},{8,16},{16,24},{24,32},{32,40},{40,48},{48,56},{56,64},{64,7... | collective-permute-start | bytes 43016 | tf_op jit(solution)/shard_map/ppermute | solution.py:24
  43.9 42.8 %collective-permute-start.2 = (bf16[1,28,256]{2,1,0:T(8,128)(2,1)}, bf16[1,28,256]{2,1,0:T(8,128)(2,1)}, u32[]{:S(2)}, u32[]{:S(2)}) collective-permute-start(bf16[1,28,256]{2,1,0:T(8,128)(2,1)} %get-tuple-element.111), channel_id=1, source_target_pairs={{0,8},{8,16},{16,24},{24,32},{32,40},{40,48},{48,56},{56,64},{64,7... | collective-permute-start | bytes 43016 | tf_op jit(solution)/shard_map/ppermute | solution.py:24
  47.0 42.4 %collective-permute-start.3 = (bf16[1,28,256]{2,1,0:T(8,128)(2,1)}, bf16[1,28,256]{2,1,0:T(8,128)(2,1)}, u32[]{:S(2)}, u32[]{:S(2)}) collective-permute-start(bf16[1,28,256]{2,1,0:T(8,128)(2,1)} %get-tuple-element.110), channel_id=1, source_target_pairs={{0,8},{8,16},{16,24},{24,32},{32,40},{40,48},{48,56},{56,64},{64,7... | collective-permute-start | bytes 43016 | tf_op jit(solution)/shard_map/ppermute | solution.py:24
  49.9 41.8 %collective-permute-start.5 = (bf16[1,28,256]{2,1,0:T(8,128)(2,1)}, bf16[1,28,256]{2,1,0:T(8,128)(2,1)}, u32[]{:S(2)}, u32[]{:S(2)}) collective-permute-start(bf16[1,28,256]{2,1,0:T(8,128)(2,1)} %get-tuple-element.109), channel_id=1, source_target_pairs={{0,1},{1,2},{2,3},{3,4},{4,5},{5,6},{6,7},{8,9},{9,10},{10,11},{11... | collective-permute-start | bytes 43016 | tf_op jit(solution)/shard_map/ppermute | solution.py:24
  54.5 40.3 %collective-permute-start.6 = (bf16[1,28,256]{2,1,0:T(8,128)(2,1)}, bf16[1,28,256]{2,1,0:T(8,128)(2,1)}, u32[]{:S(2)}, u32[]{:S(2)}) collective-permute-start(bf16[1,28,256]{2,1,0:T(8,128)(2,1)} %get-tuple-element.108), channel_id=1, source_target_pairs={{1,0},{2,1},{3,2},{4,3},{5,4},{6,5},{7,6},{9,8},{10,9},{11,10},{12... | collective-permute-start | bytes 43016 | tf_op jit(solution)/shard_map/ppermute | solution.py:24
  82.1 17.4 %collective-permute-start.7 = (bf16[1,28,256]{2,1,0:T(8,128)(2,1)S(1)}, bf16[1,28,256]{2,1,0:T(8,128)(2,1)}, u32[]{:S(2)}, u32[]{:S(2)}) collective-permute-start(bf16[1,28,256]{2,1,0:T(8,128)(2,1)S(1)} %copy-done.105), channel_id=1, source_target_pairs={{8,0},{16,8},{24,16},{32,24},{40,32},{48,40},{56,48},{64,56},{72,6... | collective-permute-start | bytes 43016 | tf_op jit(solution)/shard_map/ppermute | solution.py:24
  89.5 16.3 %collective-permute-start.10 = (bf16[1,28,256]{2,1,0:T(8,128)(2,1)S(1)}, bf16[1,28,256]{2,1,0:T(8,128)(2,1)}, u32[]{:S(2)}, u32[]{:S(2)}) collective-permute-start(bf16[1,28,256]{2,1,0:T(8,128)(2,1)S(1)} %copy-done.103), channel_id=1, source_target_pairs={{8,0},{16,8},{24,16},{32,24},{40,32},{48,40},{56,48},{64,56},{72,6... | collective-permute-start | bytes 43016 | tf_op jit(solution)/shard_map/ppermute | solution.py:24
  91.6 16.1 %collective-permute-start.26 = (bf16[1,28,256]{2,1,0:T(8,128)(2,1)}, bf16[1,28,256]{2,1,0:T(8,128)(2,1)S(1)}, u32[]{:S(2)}, u32[]{:S(2)}) collective-permute-start(bf16[1,28,256]{2,1,0:T(8,128)(2,1)} %get-tuple-element.103), channel_id=1, source_target_pairs={{0,8},{8,16},{16,24},{24,32},{32,40},{40,48},{48,56},{56,64},{64,7... | collective-permute-start | bytes 43016 | tf_op jit(solution)/shard_map/ppermute | solution.py:24
  94.8 16.9 %collective-permute-start.29 = (bf16[1,28,256]{2,1,0:T(8,128)(2,1)}, bf16[1,28,256]{2,1,0:T(8,128)(2,1)S(1)}, u32[]{:S(2)}, u32[]{:S(2)}) collective-permute-start(bf16[1,28,256]{2,1,0:T(8,128)(2,1)} %get-tuple-element.101), channel_id=1, source_target_pairs={{0,1},{1,2},{2,3},{3,4},{4,5},{5,6},{6,7},{8,9},{9,10},{10,11},{11... | collective-permute-start | bytes 43016 | tf_op jit(solution)/shard_map/ppermute | solution.py:24
  101.5 17.9 %collective-permute-start.33 = (bf16[1,28,256]{2,1,0:T(8,128)(2,1)}, bf16[1,28,256]{2,1,0:T(8,128)(2,1)S(1)}, u32[]{:S(2)}, u32[]{:S(2)}) collective-permute-start(bf16[1,28,256]{2,1,0:T(8,128)(2,1)} %get-tuple-element.98), channel_id=1, source_target_pairs={{8,0},{16,8},{24,16},{32,24},{40,32},{48,40},{56,48},{64,56},{72,6... | collective-permute-start | bytes 43016 | tf_op jit(solution)/shard_map/ppermute | solution.py:24
  105.8 18.2 %collective-permute-start.50 = (bf16[1,28,256]{2,1,0:T(8,128)(2,1)S(1)}, bf16[1,28,256]{2,1,0:T(8,128)(2,1)S(1)}, u32[]{:S(2)}, u32[]{:S(2)}) collective-permute-start(bf16[1,28,256]{2,1,0:T(8,128)(2,1)S(1)} %get-tuple-element.95), channel_id=1, source_target_pairs={{0,8},{8,16},{16,24},{24,32},{32,40},{40,48},{48,56},{56,64},{64,7... | collective-permute-start | bytes 43016 | tf_op jit(solution)/shard_map/ppermute | solution.py:24
  107.8 18.1 %collective-permute-start.53 = (bf16[1,28,256]{2,1,0:T(8,128)(2,1)S(1)}, bf16[1,28,256]{2,1,0:T(8,128)(2,1)S(1)}, u32[]{:S(2)}, u32[]{:S(2)}) collective-permute-start(bf16[1,28,256]{2,1,0:T(8,128)(2,1)S(1)} %get-tuple-element.93), channel_id=1, source_target_pairs={{0,1},{1,2},{2,3},{3,4},{4,5},{5,6},{6,7},{8,9},{9,10},{10,11},{11... | collective-permute-start | bytes 43016 | tf_op jit(solution)/shard_map/ppermute | solution.py:24
  111.7 16.1 %collective-permute-start.54 = (bf16[1,28,256]{2,1,0:T(8,128)(2,1)S(1)}, bf16[1,28,256]{2,1,0:T(8,128)(2,1)S(1)}, u32[]{:S(2)}, u32[]{:S(2)}) collective-permute-start(bf16[1,28,256]{2,1,0:T(8,128)(2,1)S(1)} %get-tuple-element.92), channel_id=1, source_target_pairs={{1,0},{2,1},{3,2},{4,3},{5,4},{6,5},{7,6},{9,8},{10,9},{11,10},{12... | collective-permute-start | bytes 43016 | tf_op jit(solution)/shard_map/ppermute | solution.py:24
  113.7 16.1 %collective-permute-start.57 = (bf16[1,28,256]{2,1,0:T(8,128)(2,1)S(1)}, bf16[1,28,256]{2,1,0:T(8,128)(2,1)S(1)}, u32[]{:S(2)}, u32[]{:S(2)}) collective-permute-start(bf16[1,28,256]{2,1,0:T(8,128)(2,1)S(1)} %get-tuple-element.90), channel_id=1, source_target_pairs={{8,0},{16,8},{24,16},{32,24},{40,32},{48,40},{56,48},{64,56},{72,6... | collective-permute-start | bytes 43016 | tf_op jit(solution)/shard_map/ppermute | solution.py:24
  124.0 36.8 %collective-permute-start.24 = (bf16[1,28,256]{2,1,0:T(8,128)(2,1)S(1)}, bf16[1,28,256]{2,1,0:T(8,128)(2,1)}, u32[]{:S(2)}, u32[]{:S(2)}) collective-permute-start(bf16[1,28,256]{2,1,0:T(8,128)(2,1)S(1)} %get-tuple-element.104), channel_id=1, source_target_pairs={{0,8},{8,16},{16,24},{24,32},{32,40},{40,48},{48,56},{56,64},{64,7... | collective-permute-start | bytes 43016 | tf_op jit(solution)/shard_map/ppermute | solution.py:24
  125.9 36.8 %collective-permute-start.27 = (bf16[1,28,256]{2,1,0:T(8,128)(2,1)S(1)}, bf16[1,28,256]{2,1,0:T(8,128)(2,1)}, u32[]{:S(2)}, u32[]{:S(2)}) collective-permute-start(bf16[1,28,256]{2,1,0:T(8,128)(2,1)S(1)} %get-tuple-element.102), channel_id=1, source_target_pairs={{0,8},{8,16},{16,24},{24,32},{32,40},{40,48},{48,56},{56,64},{64,7... | collective-permute-start | bytes 43016 | tf_op jit(solution)/shard_map/ppermute | solution.py:24
  127.9 22.6 %collective-permute-start.4 = (bf16[1,28,256]{2,1,0:T(8,128)(2,1)}, bf16[1,28,256]{2,1,0:T(8,128)(2,1)}, u32[]{:S(2)}, u32[]{:S(2)}) collective-permute-start(bf16[1,28,256]{2,1,0:T(8,128)(2,1)} %collective-permute-done.3), channel_id=1, source_target_pairs={{1,0},{2,1},{3,2},{4,3},{5,4},{6,5},{7,6},{9,8},{10,9},{11,10},{12... | collective-permute-start | bytes 43016 | tf_op jit(solution)/shard_map/ppermute | solution.py:24
  129.8 26.8 %collective-permute-start.8 = (bf16[1,28,256]{2,1,0:T(8,128)(2,1)}, bf16[1,28,256]{2,1,0:T(8,128)(2,1)}, u32[]{:S(2)}, u32[]{:S(2)}) collective-permute-start(bf16[1,28,256]{2,1,0:T(8,128)(2,1)} %collective-permute-done.7), channel_id=1, source_target_pairs={{0,1},{1,2},{2,3},{3,4},{4,5},{5,6},{6,7},{8,9},{9,10},{10,11},{11... | collective-permute-start | bytes 43016 | tf_op jit(solution)/shard_map/ppermute | solution.py:24
  133.5 33.7 %collective-permute-start.11 = (bf16[1,28,256]{2,1,0:T(8,128)(2,1)}, bf16[1,28,256]{2,1,0:T(8,128)(2,1)S(1)}, u32[]{:S(2)}, u32[]{:S(2)}) collective-permute-start(bf16[1,28,256]{2,1,0:T(8,128)(2,1)} %collective-permute-done.10), channel_id=1, source_target_pairs={{1,0},{2,1},{3,2},{4,3},{5,4},{6,5},{7,6},{9,8},{10,9},{11,10},{12... | collective-permute-start | bytes 43016 | tf_op jit(solution)/shard_map/ppermute | solution.py:24
  150.4 59.4 %collective-permute-start.31 = (bf16[1,28,256]{2,1,0:T(8,128)(2,1)}, bf16[1,28,256]{2,1,0:T(8,128)(2,1)}, u32[]{:S(2)}, u32[]{:S(2)}) collective-permute-start(bf16[1,28,256]{2,1,0:T(8,128)(2,1)} %get-tuple-element.99), channel_id=1, source_target_pairs={{8,0},{16,8},{24,16},{32,24},{40,32},{48,40},{56,48},{64,56},{72,6... | collective-permute-start | bytes 43016 | tf_op jit(solution)/shard_map/ppermute | solution.py:24
  156.7 55.2 %collective-permute-start.34 = (bf16[1,28,256]{2,1,0:T(8,128)(2,1)}, bf16[1,28,256]{2,1,0:T(8,128)(2,1)}, u32[]{:S(2)}, u32[]{:S(2)}) collective-permute-start(bf16[1,28,256]{2,1,0:T(8,128)(2,1)} %get-tuple-element.97), channel_id=1, source_target_pairs={{8,0},{16,8},{24,16},{32,24},{40,32},{48,40},{56,48},{64,56},{72,6... | collective-permute-start | bytes 43016 | tf_op jit(solution)/shard_map/ppermute | solution.py:24
  160.8 56.6 %collective-permute-start.48 = (bf16[1,28,256]{2,1,0:T(8,128)(2,1)}, bf16[1,28,256]{2,1,0:T(8,128)(2,1)}, u32[]{:S(2)}, u32[]{:S(2)}) collective-permute-start(bf16[1,28,256]{2,1,0:T(8,128)(2,1)} %get-tuple-element.96), channel_id=1, source_target_pairs={{0,8},{8,16},{16,24},{24,32},{32,40},{40,48},{48,56},{56,64},{64,7... | collective-permute-start | bytes 43016 | tf_op jit(solution)/shard_map/ppermute | solution.py:24
  162.7 58.0 %collective-permute-start.25 = (bf16[1,28,256]{2,1,0:T(8,128)(2,1)}, bf16[1,28,256]{2,1,0:T(8,128)(2,1)}, u32[]{:S(2)}, u32[]{:S(2)}) collective-permute-start(bf16[1,28,256]{2,1,0:T(8,128)(2,1)} %collective-permute-done.24), channel_id=1, source_target_pairs={{0,1},{1,2},{2,3},{3,4},{4,5},{5,6},{6,7},{8,9},{9,10},{10,11},{11... | collective-permute-start | bytes 43016 | tf_op jit(solution)/shard_map/ppermute | solution.py:24
  167.2 58.0 %collective-permute-start.28 = (bf16[1,28,256]{2,1,0:T(8,128)(2,1)}, bf16[1,28,256]{2,1,0:T(8,128)(2,1)}, u32[]{:S(2)}, u32[]{:S(2)}) collective-permute-start(bf16[1,28,256]{2,1,0:T(8,128)(2,1)} %collective-permute-done.27), channel_id=1, source_target_pairs={{1,0},{2,1},{3,2},{4,3},{5,4},{6,5},{7,6},{9,8},{10,9},{11,10},{12... | collective-permute-start | bytes 43016 | tf_op jit(solution)/shard_map/ppermute | solution.py:24
  209.8 22.4 %collective-permute-start.51 = (bf16[1,28,256]{2,1,0:T(8,128)(2,1)}, bf16[1,28,256]{2,1,0:T(8,128)(2,1)}, u32[]{:S(2)}, u32[]{:S(2)}) collective-permute-start(bf16[1,28,256]{2,1,0:T(8,128)(2,1)} %get-tuple-element.94), channel_id=1, source_target_pairs={{0,8},{8,16},{16,24},{24,32},{32,40},{40,48},{48,56},{56,64},{64,7... | collective-permute-start | bytes 43016 | tf_op jit(solution)/shard_map/ppermute | solution.py:24
  211.9 24.0 %collective-permute-start.55 = (bf16[1,28,256]{2,1,0:T(8,128)(2,1)}, bf16[1,28,256]{2,1,0:T(8,128)(2,1)}, u32[]{:S(2)}, u32[]{:S(2)}) collective-permute-start(bf16[1,28,256]{2,1,0:T(8,128)(2,1)} %get-tuple-element.91), channel_id=1, source_target_pairs={{8,0},{16,8},{24,16},{32,24},{40,32},{48,40},{56,48},{64,56},{72,6... | collective-permute-start | bytes 43016 | tf_op jit(solution)/shard_map/ppermute | solution.py:24
  217.4 20.4 %collective-permute-start.58 = (bf16[1,28,256]{2,1,0:T(8,128)(2,1)}, bf16[1,28,256]{2,1,0:T(8,128)(2,1)}, u32[]{:S(2)}, u32[]{:S(2)}) collective-permute-start(bf16[1,28,256]{2,1,0:T(8,128)(2,1)} %get-tuple-element.89), channel_id=1, source_target_pairs={{8,0},{16,8},{24,16},{32,24},{40,32},{48,40},{56,48},{64,56},{72,6... | collective-permute-start | bytes 43016 | tf_op jit(solution)/shard_map/ppermute | solution.py:24
  220.7 20.7 %collective-permute-start.32 = (bf16[1,28,256]{2,1,0:T(8,128)(2,1)}, bf16[1,28,256]{2,1,0:T(8,128)(2,1)S(1)}, u32[]{:S(2)}, u32[]{:S(2)}) collective-permute-start(bf16[1,28,256]{2,1,0:T(8,128)(2,1)} %collective-permute-done.31), channel_id=1, source_target_pairs={{0,1},{1,2},{2,3},{3,4},{4,5},{5,6},{6,7},{8,9},{9,10},{10,11},{11... | collective-permute-start | bytes 43016 | tf_op jit(solution)/shard_map/ppermute | solution.py:24
  225.2 18.2 %collective-permute-start.35 = (bf16[1,28,256]{2,1,0:T(8,128)(2,1)}, bf16[1,28,256]{2,1,0:T(8,128)(2,1)S(1)}, u32[]{:S(2)}, u32[]{:S(2)}) collective-permute-start(bf16[1,28,256]{2,1,0:T(8,128)(2,1)} %collective-permute-done.34), channel_id=1, source_target_pairs={{1,0},{2,1},{3,2},{4,3},{5,4},{6,5},{7,6},{9,8},{10,9},{11,10},{12... | collective-permute-start | bytes 43016 | tf_op jit(solution)/shard_map/ppermute | solution.py:24
  232.2 34.7 %collective-permute-start.49 = (bf16[1,28,256]{2,1,0:T(8,128)(2,1)}, bf16[1,28,256]{2,1,0:T(8,128)(2,1)}, u32[]{:S(2)}, u32[]{:S(2)}) collective-permute-start(bf16[1,28,256]{2,1,0:T(8,128)(2,1)} %collective-permute-done.48), channel_id=1, source_target_pairs={{0,1},{1,2},{2,3},{3,4},{4,5},{5,6},{6,7},{8,9},{9,10},{10,11},{11... | collective-permute-start | bytes 43016 | tf_op jit(solution)/shard_map/ppermute | solution.py:24
  235.9 33.7 %collective-permute-start.52 = (bf16[1,28,256]{2,1,0:T(8,128)(2,1)}, bf16[1,28,256]{2,1,0:T(8,128)(2,1)}, u32[]{:S(2)}, u32[]{:S(2)}) collective-permute-start(bf16[1,28,256]{2,1,0:T(8,128)(2,1)} %collective-permute-done.51), channel_id=1, source_target_pairs={{1,0},{2,1},{3,2},{4,3},{5,4},{6,5},{7,6},{9,8},{10,9},{11,10},{12... | collective-permute-start | bytes 43016 | tf_op jit(solution)/shard_map/ppermute | solution.py:24
  237.8 35.4 %collective-permute-start.56 = (bf16[1,28,256]{2,1,0:T(8,128)(2,1)}, bf16[1,28,256]{2,1,0:T(8,128)(2,1)}, u32[]{:S(2)}, u32[]{:S(2)}) collective-permute-start(bf16[1,28,256]{2,1,0:T(8,128)(2,1)} %collective-permute-done.55), channel_id=1, source_target_pairs={{0,1},{1,2},{2,3},{3,4},{4,5},{5,6},{6,7},{8,9},{9,10},{10,11},{11... | collective-permute-start | bytes 43016 | tf_op jit(solution)/shard_map/ppermute | solution.py:24
  241.5 37.0 %collective-permute-start.59 = (bf16[1,28,256]{2,1,0:T(8,128)(2,1)}, bf16[1,28,256]{2,1,0:T(8,128)(2,1)}, u32[]{:S(2)}, u32[]{:S(2)}) collective-permute-start(bf16[1,28,256]{2,1,0:T(8,128)(2,1)} %collective-permute-done.58), channel_id=1, source_target_pairs={{1,0},{2,1},{3,2},{4,3},{5,4},{6,5},{7,6},{9,8},{10,9},{11,10},{12... | collective-permute-start | bytes 43016 | tf_op jit(solution)/shard_map/ppermute | solution.py:24
  243.4 55.2 %collective-permute-start.12 = (f32[28,256]{1,0:T(8,128)}, f32[28,256]{1,0:T(8,128)}, u32[]{:S(2)}, u32[]{:S(2)}) collective-permute-start(f32[28,256]{1,0:T(8,128)} %bitcast.43), channel_id=1, source_target_pairs={{0,8},{8,16},{16,24},{24,32},{32,40},{40,48},{48,56},{56,64},{64,7... | collective-permute-start | bytes 86024 | tf_op jit(solution)/shard_map/ppermute | solution.py:24
  266.9 35.9 %collective-permute-start.14 = (f32[28,256]{1,0:T(8,128)}, f32[28,256]{1,0:T(8,128)}, u32[]{:S(2)}, u32[]{:S(2)}) collective-permute-start(f32[28,256]{1,0:T(8,128)} %bitcast.44), channel_id=1, source_target_pairs={{0,8},{8,16},{16,24},{24,32},{32,40},{40,48},{48,56},{56,64},{64,7... | collective-permute-start | bytes 86024 | tf_op jit(solution)/shard_map/ppermute | solution.py:24
  269.5 37.7 %collective-permute-start.15 = (f32[28,256]{1,0:T(8,128)}, f32[28,256]{1,0:T(8,128)}, u32[]{:S(2)}, u32[]{:S(2)}) collective-permute-start(f32[28,256]{1,0:T(8,128)} %bitcast.45), channel_id=1, source_target_pairs={{0,8},{8,16},{16,24},{24,32},{32,40},{40,48},{48,56},{56,64},{64,7... | collective-permute-start | bytes 86024 | tf_op jit(solution)/shard_map/ppermute | solution.py:24
  273.2 37.3 %collective-permute-start.17 = (f32[28,256]{1,0:T(8,128)}, f32[28,256]{1,0:T(8,128)}, u32[]{:S(2)}, u32[]{:S(2)}) collective-permute-start(f32[28,256]{1,0:T(8,128)} %bitcast.46), channel_id=1, source_target_pairs={{0,1},{1,2},{2,3},{3,4},{4,5},{5,6},{6,7},{8,9},{9,10},{10,11},{11... | collective-permute-start | bytes 86024 | tf_op jit(solution)/shard_map/ppermute | solution.py:24
  278.5 36.6 %collective-permute-start.18 = (f32[28,256]{1,0:T(8,128)}, f32[28,256]{1,0:T(8,128)}, u32[]{:S(2)}, u32[]{:S(2)}) collective-permute-start(f32[28,256]{1,0:T(8,128)} %bitcast.47), channel_id=1, source_target_pairs={{1,0},{2,1},{3,2},{4,3},{5,4},{6,5},{7,6},{9,8},{10,9},{11,10},{12... | collective-permute-start | bytes 86024 | tf_op jit(solution)/shard_map/ppermute | solution.py:24
  298.6 18.4 %collective-permute-start.19 = (f32[28,256]{1,0:T(8,128)S(1)}, f32[28,256]{1,0:T(8,128)}, u32[]{:S(2)}, u32[]{:S(2)}) collective-permute-start(f32[28,256]{1,0:T(8,128)S(1)} %bitcast.411), channel_id=1, source_target_pairs={{8,0},{16,8},{24,16},{32,24},{40,32},{48,40},{56,48},{64,56},{72,6... | collective-permute-start | bytes 86024 | tf_op jit(solution)/shard_map/ppermute | solution.py:24
  302.8 17.8 %collective-permute-start.22 = (f32[28,256]{1,0:T(8,128)S(1)}, f32[28,256]{1,0:T(8,128)}, u32[]{:S(2)}, u32[]{:S(2)}) collective-permute-start(f32[28,256]{1,0:T(8,128)S(1)} %bitcast.410), channel_id=1, source_target_pairs={{8,0},{16,8},{24,16},{32,24},{40,32},{48,40},{56,48},{64,56},{72,6... | collective-permute-start | bytes 86024 | tf_op jit(solution)/shard_map/ppermute | solution.py:24
  307.2 26.7 %collective-permute-start.21 = (f32[28,256]{1,0:T(8,128)}, f32[28,256]{1,0:T(8,128)S(1)}, u32[]{:S(2)}, u32[]{:S(2)}) collective-permute-start(f32[28,256]{1,0:T(8,128)} %bitcast.49), channel_id=1, source_target_pairs={{8,0},{16,8},{24,16},{32,24},{40,32},{48,40},{56,48},{64,56},{72,6... | collective-permute-start | bytes 86024 | tf_op jit(solution)/shard_map/ppermute | solution.py:24
  310.6 23.4 %collective-permute-start.13 = (f32[28,256]{1,0:T(8,128)}, f32[28,256]{1,0:T(8,128)S(1)}, u32[]{:S(2)}, u32[]{:S(2)}) collective-permute-start(f32[28,256]{1,0:T(8,128)} %collective-permute-done.12), channel_id=1, source_target_pairs={{0,1},{1,2},{2,3},{3,4},{4,5},{5,6},{6,7},{8,9},{9,10},{10,11},{11... | collective-permute-start | bytes 86024 | tf_op jit(solution)/shard_map/ppermute | solution.py:24
  315.1 18.9 %collective-permute-start.16 = (f32[28,256]{1,0:T(8,128)}, f32[28,256]{1,0:T(8,128)S(1)}, u32[]{:S(2)}, u32[]{:S(2)}) collective-permute-start(f32[28,256]{1,0:T(8,128)} %collective-permute-done.15), channel_id=1, source_target_pairs={{1,0},{2,1},{3,2},{4,3},{5,4},{6,5},{7,6},{9,8},{10,9},{11,10},{12... | collective-permute-start | bytes 86024 | tf_op jit(solution)/shard_map/ppermute | solution.py:24
  317.0 17.0 %collective-permute-start.20 = (f32[28,256]{1,0:T(8,128)}, f32[28,256]{1,0:T(8,128)S(1)}, u32[]{:S(2)}, u32[]{:S(2)}) collective-permute-start(f32[28,256]{1,0:T(8,128)} %collective-permute-done.19), channel_id=1, source_target_pairs={{0,1},{1,2},{2,3},{3,4},{4,5},{5,6},{6,7},{8,9},{9,10},{10,11},{11... | collective-permute-start | bytes 86024 | tf_op jit(solution)/shard_map/ppermute | solution.py:24
  383.8 26.3 %collective-permute-start.36 = (f32[28,256]{1,0:T(8,128)}, f32[28,256]{1,0:T(8,128)}, u32[]{:S(2)}, u32[]{:S(2)}) collective-permute-start(f32[28,256]{1,0:T(8,128)} %bitcast.81), channel_id=1, source_target_pairs={{0,8},{8,16},{16,24},{24,32},{32,40},{40,48},{48,56},{56,64},{64,7... | collective-permute-start | bytes 86024 | tf_op jit(solution)/shard_map/ppermute | solution.py:24
  387.3 27.0 %collective-permute-start.38 = (f32[28,256]{1,0:T(8,128)}, f32[28,256]{1,0:T(8,128)}, u32[]{:S(2)}, u32[]{:S(2)}) collective-permute-start(f32[28,256]{1,0:T(8,128)} %bitcast.82), channel_id=1, source_target_pairs={{0,8},{8,16},{16,24},{24,32},{32,40},{40,48},{48,56},{56,64},{64,7... | collective-permute-start | bytes 86024 | tf_op jit(solution)/shard_map/ppermute | solution.py:24
  390.8 30.0 %collective-permute-start.39 = (f32[28,256]{1,0:T(8,128)}, f32[28,256]{1,0:T(8,128)}, u32[]{:S(2)}, u32[]{:S(2)}) collective-permute-start(f32[28,256]{1,0:T(8,128)} %bitcast.83), channel_id=1, source_target_pairs={{0,8},{8,16},{16,24},{24,32},{32,40},{40,48},{48,56},{56,64},{64,7... | collective-permute-start | bytes 86024 | tf_op jit(solution)/shard_map/ppermute | solution.py:24
  395.4 28.8 %collective-permute-start.41 = (f32[28,256]{1,0:T(8,128)}, f32[28,256]{1,0:T(8,128)}, u32[]{:S(2)}, u32[]{:S(2)}) collective-permute-start(f32[28,256]{1,0:T(8,128)} %bitcast.84), channel_id=1, source_target_pairs={{0,1},{1,2},{2,3},{3,4},{4,5},{5,6},{6,7},{8,9},{9,10},{10,11},{11... | collective-permute-start | bytes 86024 | tf_op jit(solution)/shard_map/ppermute | solution.py:24
  400.8 27.9 %collective-permute-start.42 = (f32[28,256]{1,0:T(8,128)S(1)}, f32[28,256]{1,0:T(8,128)}, u32[]{:S(2)}, u32[]{:S(2)}) collective-permute-start(f32[28,256]{1,0:T(8,128)S(1)} %bitcast.409), channel_id=1, source_target_pairs={{1,0},{2,1},{3,2},{4,3},{5,4},{6,5},{7,6},{9,8},{10,9},{11,10},{12... | collective-permute-start | bytes 86024 | tf_op jit(solution)/shard_map/ppermute | solution.py:24
  410.1 20.6 %collective-permute-start.43 = (f32[28,256]{1,0:T(8,128)}, f32[28,256]{1,0:T(8,128)}, u32[]{:S(2)}, u32[]{:S(2)}) collective-permute-start(f32[28,256]{1,0:T(8,128)} %bitcast.86), channel_id=1, source_target_pairs={{8,0},{16,8},{24,16},{32,24},{40,32},{48,40},{56,48},{64,56},{72,6... | collective-permute-start | bytes 86024 | tf_op jit(solution)/shard_map/ppermute | solution.py:24
  414.3 20.0 %collective-permute-start.46 = (f32[28,256]{1,0:T(8,128)}, f32[28,256]{1,0:T(8,128)}, u32[]{:S(2)}, u32[]{:S(2)}) collective-permute-start(f32[28,256]{1,0:T(8,128)} %bitcast.88), channel_id=1, source_target_pairs={{8,0},{16,8},{24,16},{32,24},{40,32},{48,40},{56,48},{64,56},{72,6... | collective-permute-start | bytes 86024 | tf_op jit(solution)/shard_map/ppermute | solution.py:24
  420.9 23.2 %collective-permute-start.45 = (f32[28,256]{1,0:T(8,128)}, f32[28,256]{1,0:T(8,128)}, u32[]{:S(2)}, u32[]{:S(2)}) collective-permute-start(f32[28,256]{1,0:T(8,128)} %bitcast.87), channel_id=1, source_target_pairs={{8,0},{16,8},{24,16},{32,24},{40,32},{48,40},{56,48},{64,56},{72,6... | collective-permute-start | bytes 86024 | tf_op jit(solution)/shard_map/ppermute | solution.py:24
  424.2 20.7 %collective-permute-start.37 = (f32[28,256]{1,0:T(8,128)}, f32[28,256]{1,0:T(8,128)}, u32[]{:S(2)}, u32[]{:S(2)}) collective-permute-start(f32[28,256]{1,0:T(8,128)} %collective-permute-done.36), channel_id=1, source_target_pairs={{0,1},{1,2},{2,3},{3,4},{4,5},{5,6},{6,7},{8,9},{9,10},{10,11},{11... | collective-permute-start | bytes 86024 | tf_op jit(solution)/shard_map/ppermute | solution.py:24
  428.7 16.9 %collective-permute-start.40 = (f32[28,256]{1,0:T(8,128)}, f32[28,256]{1,0:T(8,128)}, u32[]{:S(2)}, u32[]{:S(2)}) collective-permute-start(f32[28,256]{1,0:T(8,128)} %collective-permute-done.39), channel_id=1, source_target_pairs={{1,0},{2,1},{3,2},{4,3},{5,4},{6,5},{7,6},{9,8},{10,9},{11,10},{12... | collective-permute-start | bytes 86024 | tf_op jit(solution)/shard_map/ppermute | solution.py:24
  430.7 15.8 %collective-permute-start.44 = (f32[28,256]{1,0:T(8,128)}, f32[28,256]{1,0:T(8,128)}, u32[]{:S(2)}, u32[]{:S(2)}) collective-permute-start(f32[28,256]{1,0:T(8,128)} %collective-permute-done.43), channel_id=1, source_target_pairs={{0,1},{1,2},{2,3},{3,4},{4,5},{5,6},{6,7},{8,9},{9,10},{10,11},{11... | collective-permute-start | bytes 86024 | tf_op jit(solution)/shard_map/ppermute | solution.py:24
  495.7 134.1 %collective-permute-start.60 = (f32[28,256]{1,0:T(8,128)}, f32[28,256]{1,0:T(8,128)}, u32[]{:S(2)}, u32[]{:S(2)}) collective-permute-start(f32[28,256]{1,0:T(8,128)} %bitcast.119), channel_id=1, source_target_pairs={{0,8},{8,16},{16,24},{24,32},{32,40},{40,48},{48,56},{56,64},{64,7... | collective-permute-start | bytes 86024 | tf_op jit(solution)/shard_map/ppermute | solution.py:24
  499.3 134.9 %collective-permute-start.62 = (f32[28,256]{1,0:T(8,128)}, f32[28,256]{1,0:T(8,128)}, u32[]{:S(2)}, u32[]{:S(2)}) collective-permute-start(f32[28,256]{1,0:T(8,128)} %bitcast.120), channel_id=1, source_target_pairs={{0,8},{8,16},{16,24},{24,32},{32,40},{40,48},{48,56},{56,64},{64,7... | collective-permute-start | bytes 86024 | tf_op jit(solution)/shard_map/ppermute | solution.py:24
  502.8 135.7 %collective-permute-start.63 = (f32[28,256]{1,0:T(8,128)}, f32[28,256]{1,0:T(8,128)}, u32[]{:S(2)}, u32[]{:S(2)}) collective-permute-start(f32[28,256]{1,0:T(8,128)} %bitcast.121), channel_id=1, source_target_pairs={{0,8},{8,16},{16,24},{24,32},{32,40},{40,48},{48,56},{56,64},{64,7... | collective-permute-start | bytes 86024 | tf_op jit(solution)/shard_map/ppermute | solution.py:24
  506.3 134.9 %collective-permute-start.65 = (f32[28,256]{1,0:T(8,128)}, f32[28,256]{1,0:T(8,128)}, u32[]{:S(2)}, u32[]{:S(2)}) collective-permute-start(f32[28,256]{1,0:T(8,128)} %bitcast.122), channel_id=1, source_target_pairs={{0,1},{1,2},{2,3},{3,4},{4,5},{5,6},{6,7},{8,9},{9,10},{10,11},{11... | collective-permute-start | bytes 86024 | tf_op jit(solution)/shard_map/ppermute | solution.py:24
  510.8 133.6 %collective-permute-start.66 = (f32[28,256]{1,0:T(8,128)S(1)}, f32[28,256]{1,0:T(8,128)}, u32[]{:S(2)}, u32[]{:S(2)}) collective-permute-start(f32[28,256]{1,0:T(8,128)S(1)} %bitcast.408), channel_id=1, source_target_pairs={{1,0},{2,1},{3,2},{4,3},{5,4},{6,5},{7,6},{9,8},{10,9},{11,10},{12... | collective-permute-start | bytes 86024 | tf_op jit(solution)/shard_map/ppermute | solution.py:24
  629.8 16.5 %collective-permute-start.67 = (f32[28,256]{1,0:T(8,128)}, f32[28,256]{1,0:T(8,128)}, u32[]{:S(2)}, u32[]{:S(2)}) collective-permute-start(f32[28,256]{1,0:T(8,128)} %bitcast.124), channel_id=1, source_target_pairs={{8,0},{16,8},{24,16},{32,24},{40,32},{48,40},{56,48},{64,56},{72,6... | collective-permute-start | bytes 86024 | tf_op jit(solution)/shard_map/ppermute | solution.py:24
  634.1 15.9 %collective-permute-start.70 = (f32[28,256]{1,0:T(8,128)}, f32[28,256]{1,0:T(8,128)}, u32[]{:S(2)}, u32[]{:S(2)}) collective-permute-start(f32[28,256]{1,0:T(8,128)} %bitcast.126), channel_id=1, source_target_pairs={{8,0},{16,8},{24,16},{32,24},{40,32},{48,40},{56,48},{64,56},{72,6... | collective-permute-start | bytes 86024 | tf_op jit(solution)/shard_map/ppermute | solution.py:24
  638.5 21.3 %collective-permute-start.69 = (f32[28,256]{1,0:T(8,128)}, f32[28,256]{1,0:T(8,128)S(1)}, u32[]{:S(2)}, u32[]{:S(2)}) collective-permute-start(f32[28,256]{1,0:T(8,128)} %bitcast.125), channel_id=1, source_target_pairs={{8,0},{16,8},{24,16},{32,24},{40,32},{48,40},{56,48},{64,56},{72,6... | collective-permute-start | bytes 86024 | tf_op jit(solution)/shard_map/ppermute | solution.py:24
  641.3 18.6 %collective-permute-start.61 = (f32[28,256]{1,0:T(8,128)}, f32[28,256]{1,0:T(8,128)S(1)}, u32[]{:S(2)}, u32[]{:S(2)}) collective-permute-start(f32[28,256]{1,0:T(8,128)} %collective-permute-done.60), channel_id=1, source_target_pairs={{0,1},{1,2},{2,3},{3,4},{4,5},{5,6},{6,7},{8,9},{9,10},{10,11},{11... | collective-permute-start | bytes 86024 | tf_op jit(solution)/shard_map/ppermute | solution.py:24
  (162 other events, 2269.7 us)
